TPU v7x, 128 devices: a whole 4x4x4 slice. The times are simulated.
128 devices in a mesh: dp: 2 (over x_lo), seq: 16 (over z, y), mp: 4 (over x_hi, core).
Axes of the slice: x: 4 (x_hi: 2, x_lo: 2; x = x_hi * 2 + x_lo), y: 4, z: 4, core: 2. Of those that a mesh axis runs over, the one named last changes fastest.
Arguments:
- shortening_input: bfloat16 [2, 32768, 2048], P('dp', ('seq', 'mp')), may hold values from -16 to 16
- coarse_grad: bfloat16 [2, 8192, 4096], P('dp', 'seq', 'mp'), may hold values from -6 to 6
- weight_copy: bfloat16 [2, 4096, 4096], P('dp', None, 'mp'), may hold values from -0.0625 to 0.0625
- master: float32 [2, 4096, 4096], P('dp', 'seq', 'mp'), may hold values from -3 to 3
- moment: float32 [2, 4096, 4096], P('dp', 'seq', 'mp'), may hold values from -3 to 3
- second: float32 [2, 4096, 4096], P('dp', 'seq', 'mp'), may hold values from 0.05 to 5
Outputs:
- act_grad: bfloat16 [2, 32768, 2048], P('dp', ('seq', 'mp'))
- new_master: float32 [2, 4096, 4096], P('dp', 'seq', 'mp')
- new_moment: float32 [2, 4096, 4096], P('dp', 'seq', 'mp')
- new_second: float32 [2, 4096, 4096], P('dp', 'seq', 'mp')
- new_weight: bfloat16 [2, 4096, 4096], P(None, 'seq', 'mp')
All inputs are finite; a program needn't handle non-finite values.
Results may differ from a plain program's by a relative error of at most 0.009.
Values may be sent and summed in bfloat16 or wider, within the bound.
A program may use at most 128 MiB of HBM per device.

v0:
```python
import math

import jax
import jax.numpy as jnp
from jax import lax
from jax.sharding import PartitionSpec as P

SHORT = 4


first_beta = 0.9
second_beta = 0.95
first_fix = 1.0 - 0.9**10
second_fix = 1.0 - 0.95**10
adam_eps = 1e-08
learn_rate = 0.05
weight_decay = 0.1


def shifted(value, axis, steps):
    count = lax.axis_size(axis)
    initial, last = (max(0, -steps), min(count, count - steps))
    return lax.ppermute(value, axis, [(source, source + steps) for source in range(initial, last)])


def per_device(shortening_input, coarse_grad, weight_copy, master, moment, second):
    fine_rows = shortening_input[0]
    rows_dev = fine_rows.shape[0]
    features = fine_rows.shape[1]
    grad_cols = coarse_grad[0]
    coarse_rows = grad_cols.shape[0]
    wide_rows = SHORT * features
    whole_copy = lax.all_gather(weight_copy, "dp", axis=0, tiled=True)
    weights = whole_copy.reshape(wide_rows, whole_copy.shape[2])
    summed = (
        lax.psum_scatter(
            lax.dot_general(
                grad_cols, weights, (((1,), (1,)), ((), ())), preferred_element_type=jnp.float32
            ).astype(jnp.bfloat16),
            "mp",
            scatter_dimension=0,
            tiled=True,
        )
        .astype(jnp.float32)
        .reshape(rows_dev, features)
    )
    later_rows = shifted(summed[: SHORT - 1], ("seq", "mp"), -1)
    act_grad = jnp.concatenate([summed[SHORT - 1 :], later_rows], axis=0).astype(jnp.bfloat16)
    gathered = lax.all_gather(fine_rows, "mp", axis=0, tiled=True).reshape(coarse_rows, wide_rows)
    owned_rows = lax.psum_scatter(
        lax.dot_general(
            gathered, grad_cols, (((0,), (0,)), ((), ())), preferred_element_type=jnp.float32
        ).astype(jnp.bfloat16),
        ("dp", "seq"),
        scatter_dimension=0,
        tiled=True,
    ).astype(jnp.float32)
    grad_scale = 1.0 / math.sqrt(lax.axis_size("dp") * coarse_rows * lax.axis_size("seq"))
    gradient = (owned_rows * grad_scale).reshape(master.shape)
    new_moment = first_beta * moment + (1.0 - first_beta) * gradient
    new_second = second_beta * second + (1.0 - second_beta) * gradient * gradient
    step_ratio = new_moment / first_fix / (jnp.sqrt(new_second / second_fix) + adam_eps)
    new_master = master - learn_rate * (step_ratio + weight_decay * master)
    new_weight = lax.all_gather(new_master.astype(jnp.bfloat16), "dp", axis=0, tiled=True)
    return (act_grad[None], new_master, new_moment, new_second, new_weight)


def solution(mesh):
    return jax.shard_map(
        per_device,
        mesh=mesh,
        in_specs=(
            P("dp", ("seq", "mp"), None),
            P("dp", "seq", "mp"),
            P("dp", None, "mp"),
            P("dp", "seq", "mp"),
            P("dp", "seq", "mp"),
            P("dp", "seq", "mp"),
        ),
        out_specs=(
            P("dp", ("seq", "mp"), None),
            P("dp", "seq", "mp"),
            P("dp", "seq", "mp"),
            P("dp", "seq", "mp"),
            P(None, "seq", "mp"),
        ),
        check_vma=False,
    )
```

profile of v0, /device:TPU:1, one launch (start us, length us, event | category | flops | bytes accessed | tf_op | source)
XLA Modules:
  0.0 598.7 jit_solution(8087881129983664939)
XLA Ops:
  7.2 0.0 copy-start
  7.2 0.0 all-gather.9.cloned.1.call-start
  7.2 0.7 all-gather.9.cloned.1.call-update
  7.9 0.0 all-gather.5.cloned.1.call-start
  8.0 0.7 all-gather.5.cloned.1.call-update
  8.7 0.0 reduce-scatter.5.cloned.1.call-start
  8.7 66.9 %all-gather.9.cloned.1.call-done = bf16[1,2048,2048]{2,1,0:T(8,128)(2,1)} async-done(((bf16[1,512,2048]{2,1,0:T(8,128)(2,1)}), bf16[1,2048,2048]{2,1,0:T(8,128)(2,1)}) %all-gather.9.cloned.1.call-update) | async-done | bytes 8388624 | tf_op jit(solution)/shard_map/all_gather | solution.py:49
  75.6 15.1 %reshape.57 = bf16[512,8192]{1,0:T(8,128)(2,1)} reshape(bf16[1,2048,2048]{2,1,0:T(8,128)(2,1)} %all-gather.9.cloned.1.call-done) | data formatting | bytes 16777216 | tf_op jit(solution)/shard_map/reshape | solution.py:49
  90.7 0.0 copy-done
  90.7 17.8 %convolution_convert_fusion = bf16[8192,1024]{1,0:T(8,128)(2,1)} fusion(bf16[512,8192]{1,0:T(8,128)(2,1)} %reshape.57, bf16[1,512,1024]{2,1,0:T(8,128)(2,1)S(1)} %copy-done), kind=kOutput, calls=%fused_computation | convolution fusion | flops 8598323200 | bytes 26214400 | tf_op jit(solution)/shard_map/dot_general | solution.py:51
  108.4 0.0 reduce-scatter.5.cloned.1.call-update
  108.4 0.0 reduce-scatter.3.cloned.1.call-start
  108.5 169.0 %all-gather.5.cloned.1.call-done = bf16[2,4096,1024]{2,1,0:T(8,128)(2,1)} async-done(((bf16[1,4096,1024]{2,1,0:T(8,128)(2,1)}), bf16[2,4096,1024]{2,1,0:T(8,128)(2,1)}) %all-gather.5.cloned.1.call-update) | async-done | bytes 16777232 | tf_op jit(solution)/shard_map/all_gather | solution.py:33
  277.5 29.6 %convolution_convert_fusion.1 = bf16[512,8192]{1,0:T(8,128)(2,1)} fusion(bf16[8192,1024]{1,0:T(8,128)(2,1)} %bitcast.24, bf16[1,512,1024]{2,1,0:T(8,128)(2,1)S(1)} %copy-done), kind=kOutput, calls=%fused_computation.1 | convolution fusion | flops 8594128896 | bytes 26214400 | tf_op jit(solution)/shard_map/dot_general | solution.py:37
  307.1 0.0 copy-start.2
  307.1 0.0 copy-start.3
  307.1 0.0 reduce-scatter.3.cloned.1.call-update
  307.1 0.0 all-gather.7.cloned.1.call-start
  307.2 160.9 %reduce-scatter.5.cloned.1.call-done = bf16[256,1024]{1,0:T(8,128)(2,1)} async-done(((bf16[8192,1024]{1,0:T(8,128)(2,1)}), bf16[256,1024]{1,0:T(8,128)(2,1)}) %reduce-scatter.5.cloned.1.call-update) | async-done | bytes 524304 | tf_op jit(solution)/shard_map/reduce_scatter | solution.py:50
  468.1 0.0 copy-done.2
  468.1 0.0 copy-done.3
  468.1 0.0 copy-start.1
  468.1 3.9 fusion.7
  472.0 0.0 all-gather.7.cloned.1.call-update
  472.0 92.6 %reduce-scatter.3.cloned.1.call-done = bf16[128,8192]{1,0:T(8,128)(2,1)} async-done(((bf16[512,8192]{1,0:T(8,128)(2,1)}), bf16[128,8192]{1,0:T(8,128)(2,1)}) %reduce-scatter.3.cloned.1.call-update) | async-done | bytes 2097168 | tf_op jit(solution)/shard_map/reduce_scatter | solution.py:36
  564.5 3.4 reshape.56
  567.9 2.7 collective-permute-start
  570.7 0.5 slice_bitcast_fusion
  571.2 3.3 collective-permute-done
  574.5 1.5 pad_maximum_fusion
  576.0 13.9 %all-gather.7.cloned.1.call-done = bf16[2,256,1024]{2,1,0:T(8,128)(2,1)} async-done(((bf16[1,256,1024]{2,1,0:T(8,128)(2,1)}), bf16[2,256,1024]{2,1,0:T(8,128)(2,1)}) %all-gather.7.cloned.1.call-update) | async-done | bytes 1048592 | tf_op jit(solution)/shard_map/all_gather | solution.py:64
  589.9 2.3 copy.12
  592.2 0.0 copy-done.1
  (1 shorter events, 0.0 us)
Async XLA Ops:
  7.2 83.5 %copy-start = (bf16[1,512,1024]{2,1,0:T(8,128)(2,1)S(1)}, bf16[1,512,1024]{2,1,0:T(8,128)(2,1)}, u32[]{:S(2)}) copy-start(bf16[1,512,1024]{2,1,0:T(8,128)(2,1)} %param.7) | copy-start | bytes 3145732
  7.2 68.4 %all-gather.9.cloned.1.call-start = ((), (), s32[]{:S(2)}) async-start(), calls=%async_computation.6 | async-start | bytes 10485760 | tf_op jit(solution)/shard_map/all_gather | solution.py:49
  7.9 269.6 %all-gather.5.cloned.1.call-start = ((), (), s32[]{:S(2)}) async-start(), calls=%async_computation.2 | async-start | bytes 25165824 | tf_op jit(solution)/shard_map/all_gather | solution.py:33
  8.7 459.4 %reduce-scatter.5.cloned.1.call-start = ((), (), s32[]{:S(2)}) async-start(), calls=%async_computation.4 | async-start | bytes 17301504 | tf_op jit(solution)/shard_map/reduce_scatter | solution.py:50
  108.4 456.1 %reduce-scatter.3.cloned.1.call-start = ((), (), s32[]{:S(2)}) async-start(), calls=%async_computation.3 | async-start | bytes 10485760 | tf_op jit(solution)/shard_map/reduce_scatter | solution.py:36
  307.1 161.0 %copy-start.2 = (f32[1,256,1024]{2,1,0:T(8,128)S(1)}, f32[1,256,1024]{2,1,0:T(8,128)}, u32[]{:S(2)}) copy-start(f32[1,256,1024]{2,1,0:T(8,128)} %param.9) | copy-start | bytes 3145732
  307.1 161.0 %copy-start.3 = (f32[1,256,1024]{2,1,0:T(8,128)S(1)}, f32[1,256,1024]{2,1,0:T(8,128)}, u32[]{:S(2)}) copy-start(f32[1,256,1024]{2,1,0:T(8,128)} %param.10) | copy-start | bytes 3145732
  307.1 282.8 %all-gather.7.cloned.1.call-start = ((), (), s32[]{:S(2)}) async-start(), calls=%async_computation.5 | async-start | bytes 1572864 | tf_op jit(solution)/shard_map/all_gather | solution.py:64
  468.1 124.1 %copy-start.1 = (bf16[1,512,1024]{2,1,0:T(8,128)(2,1)S(1)}, bf16[1,512,1024]{2,1,0:T(8,128)(2,1)}, u32[]{:S(2)}) copy-start(bf16[1,512,1024]{2,1,0:T(8,128)(2,1)} %param.7) | copy-start | bytes 3145732
  567.9 6.6 %collective-permute-start = (bf16[3,2048]{1,0:T(4,128)(2,1)S(1)}, bf16[3,2048]{1,0:T(4,128)(2,1)S(1)}, u32[]{:S(2)}, u32[]{:S(2)}) collective-permute-start(bf16[3,2048]{1,0:T(4,128)(2,1)S(1)} %slice.18), channel_id=1, source_target_pairs={{1,0},{2,1},{3,2},{4,3},{5,4},{6,5},{7,6},{8,7},{9,8},{10,9},{11,1... | collective-permute-start | bytes 36872 | tf_op jit(solution)/shard_map/ppermute | solution.py:23
Sparse Core Ops, SparseCore 0:
  9.7 65.8 all-gather.8
  77.2 200.2 all-gather.4
  279.9 188.1 reduce-scatter.4
  470.6 93.8 reduce-scatter.2
  566.6 23.2 all-gather.6
where the time goes:
time: 599 us
  waiting for transfers between devices  508 us (85%)
  matrix products  47.4 us (8%)
  local copies, waits for them, and re-layouts  21.2 us (4%)
  between operations  13.8 us (2%)
    all_gather x1, waiting for transfers between devices, per_device(): whole_copy = lax.all_gather(weight_copy, 'dp', axis=0, tiled=True)  169 us
    reduce_scatter x1, waiting for transfers between devices, per_device(): lax.psum_scatter(lax.dot_general(gathered, grad_cols, (((0,), (0,)), ((),...  161 us
    reduce_scatter x1, waiting for transfers between devices, per_device(): lax.psum_scatter(lax.dot_general(grad_cols, weights, (((1,), (1,)), ((),...  92.6 us
    all_gather x1, waiting for transfers between devices, per_device(): lax.all_gather(fine_rows, 'mp', axis=0, tiled=True)  66.9 us
    dot_general x1, matrix products, per_device(): lax.dot_general(grad_cols, weights, (((1,), (1,)), ((), ())), preferred_e...  29.6 us
    dot_general x1, matrix products, per_device(): lax.dot_general(gathered, grad_cols, (((0,), (0,)), ((), ())), preferred_...  17.8 us
    reshape x1, local copies, waits for them, and re-layouts, per_device(): lax.all_gather(fine_rows, 'mp', axis=0, tiled=True)  15.1 us
    all_gather x1, waiting for transfers between devices, per_device(): lax.all_gather(new_master.astype(jnp.bfloat16), 'dp', axis=0, tiled=True)  13.9 us
  transfers between devices with their start and end apart: 6, of which 6 were waited for; matrix products, arithmetic and copies ran while one was open for 12% of the time, Pallas kernels for 0%

commit v1 on v0

v1 whole, which is shorter than its diff:
```python
import functools
import math

import jax
import jax.numpy as jnp
from jax import lax
from jax.experimental import pallas as pl
from jax.experimental.pallas import tpu as pltpu
from jax.sharding import PartitionSpec as P

MESH = pl.DeviceIdType.MESH
SHORT = 4
SIDE = 4

first_beta = 0.9
second_beta = 0.95
first_fix = 1.0 - 0.9**10
second_fix = 1.0 - 0.95**10
adam_eps = 1e-08
learn_rate = 0.05
weight_decay = 0.1

COPIES = 80
LOCALS = 16

F32 = jnp.float32
BF16 = jnp.bfloat16


def kernel(
    scale, x_hbm, g_hbm, w_hbm, ma_hbm, mo_hbm, se_hbm,
    act_hbm, nm_hbm, nmo_hbm, ns_hbm, nw_hbm,
    xf, xall, x2t, xrel, g2, g2s, wown, wsib, pbuf, actr, arel, rbuf,
    dwp, r1, r2, st, r3, r4, ma, mo, se, nwb, bsend, brecv,
    send_sem, recv_sem, local_sem,
):
    d = lax.axis_index("dp")
    s = lax.axis_index("seq")
    m = lax.axis_index("mp")
    z, y = s // SIDE, s % SIDE
    h, c = m // 2, m % 2
    od, oh, oc = 1 - d, 1 - h, 1 - c

    def near(dd, hh, cc):
        return {"dp": dd, "mp": 2 * hh + cc}

    def slot(dd, hh, cc):
        return 4 * dd + 2 * hh + cc

    me = slot(d, h, c)
    sibling = near(d, h, oc)
    intra, intra_o = near(od, h, c), near(od, h, oc)
    inter, inter_o = near(od, oh, c), near(od, oh, oc)

    def at_seq(zz, yy):
        return {"seq": zz * SIDE + yy}

    up = lambda v: (v + 1) % SIDE
    down = lambda v: (v + SIDE - 1) % SIDE
    across = lambda v: (v + 2) % SIDE
    zp, zm = at_seq(up(z), y), at_seq(down(z), y)
    yp, ym = at_seq(z, up(y)), at_seq(z, down(y))
    total = 64
    place = s * 4 + m
    before = (place + total - 1) % total
    after = (place + 1) % total
    prev_dev = {"seq": before // 4, "mp": before % 4}
    next_dev = {"seq": after // 4, "mp": after % 4}

    sent, ids, local_ids = [], {}, {}

    def send(name, src, dst, device):
        i = ids.setdefault(name, len(ids))
        copy = pltpu.make_async_remote_copy(
            src_ref=src, dst_ref=dst, send_sem=send_sem.at[i], recv_sem=recv_sem.at[i],
            device_id=device, device_id_type=MESH,
        )
        copy.start()
        sent.append(copy)

    def arrived(name, dst):
        i = ids.setdefault(name, len(ids))
        pltpu.make_async_remote_copy(
            src_ref=dst, dst_ref=dst, send_sem=send_sem.at[i], recv_sem=recv_sem.at[i],
            device_id=sibling, device_id_type=MESH,
        ).wait_recv()

    def local(name, src, dst):
        copy = pltpu.make_async_copy(src, dst, local_sem.at[local_ids.setdefault(name, len(local_ids))])
        copy.start()
        return copy

    in_x = local("x", x_hbm, xf)
    in_g = local("g", g_hbm, g2.at[d])
    in_w = local("w", w_hbm.at[c], wown)
    in_ma = local("ma", ma_hbm, ma)
    in_mo = local("mo", mo_hbm, mo)
    in_se = local("se", se_hbm, se)

    barrier = pltpu.get_barrier_semaphore()
    partners = (sibling, intra, intra_o, inter, inter_o, zp, zm, yp, ym, prev_dev, next_dev)
    for device in partners:
        pl.semaphore_signal(barrier, inc=1, device_id=device, device_id_type=MESH)
    pl.semaphore_wait(barrier, len(partners))

    send("G0", g_hbm, g2.at[d], intra)
    send("G1", g_hbm, g2s.at[d], sibling)
    send("W", w_hbm.at[oc], wsib, sibling)

    in_x.wait()

    def turn(i, carry):
        p, tile = i // 4, i % 4
        rows = lax.broadcasted_iota(jnp.int32, (128, 512), 0)
        cols = lax.broadcasted_iota(jnp.int32, (128, 512), 1)
        pick = jnp.where(cols == 4 * rows + p, 1.0, 0.0).astype(BF16)
        got = jnp.dot(pick, xf[:, pl.ds(pl.multiple_of(tile * 512, 512), 512)], preferred_element_type=F32)
        turned = got.T.astype(BF16)
        for j in range(4):
            owner = (p % 2) * 8 + tile * 2 + j // 2
            where = owner if j % 2 == 0 else 16 + (owner % SIDE) * SIDE + owner // SIDE
            for ch in range(2):
                xall[p // 2, ch, where] = turned[j * 128 + ch * 64:j * 128 + ch * 64 + 64]
        return carry

    lax.fori_loop(0, 16, turn, 0)
    own_x = local("xown", xall.at[d], x2t.at[me])
    first, second = pl.ds(0, 16), pl.ds(16, 16)

    def start_x(ch):
        tag = str(ch)
        send("Xa" + tag, xall.at[d, ch, first], xrel.at[ch, 0], intra)
        send("Xb" + tag, xall.at[d, ch, second], xrel.at[ch, 1], inter)
        send("Xd" + tag, xall.at[od, ch], x2t.at[me, ch], inter)
        send("Xc" + tag, xall.at[od, ch], x2t.at[me, ch], intra)
        send("Xe" + tag, xall.at[d, ch], x2t.at[me, ch], sibling)

    def relay_b(ch):
        arrived("Xb" + str(ch), xrel.at[ch, 1])
        send("Xb2" + str(ch), xrel.at[ch, 1], x2t.at[slot(od, oh, c), ch, second], intra)

    def relay_a(ch):
        arrived("Xa" + str(ch), xrel.at[ch, 0])
        send("Xa2" + str(ch), xrel.at[ch, 0], x2t.at[slot(od, h, c), ch, first], inter)

    def pass_on(name, ch, dst):
        arrived(name + str(ch), dst)
        send("F" + name + str(ch), dst, dst, sibling)

    def passed(name, ch, dst):
        arrived("F" + name + str(ch), dst)

    def act_half(dd):
        def step(t, carry):
            outs = pl.ds(pl.multiple_of(t * 256, 256), 256)
            dims = (((1,), (1,)), ((), ()))
            part = lax.dot_general(g2[dd], wown[outs, :], dims, preferred_element_type=F32)
            part += lax.dot_general(g2s[dd], wsib[outs, :], dims, preferred_element_type=F32)
            pbuf[dd, :, :, outs] = part.astype(BF16).reshape(4, 128, 256)
            return carry

        lax.fori_loop(0, 8, step, 0)

    def grad_tile(ch, group_a, group_b):
        tile_a, tile_b = pl.ds(4 * group_a, 4), pl.ds(16 + 4 * group_b, 4)

        def step(t, carry):
            cols = pl.ds(pl.multiple_of(t * 256, 256), 256)
            left = jnp.concatenate(
                [
                    jnp.concatenate([x2t[k, ch, tile].reshape(256, 128) for k in range(8)], axis=1)
                    for tile in (tile_a, tile_b)
                ],
                axis=0,
            )
            right = jnp.concatenate([g2[0, :, cols], g2[1, :, cols]], axis=0)
            part = jnp.dot(left, right, preferred_element_type=F32).astype(BF16).reshape(2, 4, 64, 256)
            dwp[ch, 0, group_a, :, :, cols] = part[0]
            dwp[ch, 1, group_b, :, :, cols] = part[1]
            return carry

        lax.fori_loop(0, 4, step, 0)

    def wide(v):
        return v.astype(F32)

    halves = (("A", z, y, zp, zm, yp, ym), ("B", y, z, yp, ym, zp, zm))

    def reduce_1(ch):
        for i, (tag, a1, a2, p1, m1, p2, m2) in enumerate(halves):
            tag += str(ch)
            send(tag + "1p", dwp.at[ch, i, across(a1), pl.ds(0, 2)], r1.at[ch, i, 0], p1)
            send(tag + "1m", dwp.at[ch, i, across(a1), pl.ds(2, 2)], r1.at[ch, i, 1], m1)

    def reduce_2(ch):
        for i, (tag, a1, a2, p1, m1, p2, m2) in enumerate(halves):
            tag += str(ch)
            arrived(tag + "1p", r1.at[ch, i, 0])
            for j in range(2):
                dwp[ch, i, up(a1), j] = (wide(dwp[ch, i, up(a1), j]) + wide(r1[ch, i, 0, j])).astype(BF16)
            send(tag + "2p", dwp.at[ch, i, up(a1)], r2.at[ch, i, 0], p1)
            arrived(tag + "1m", r1.at[ch, i, 1])
            for j in range(2):
                dwp[ch, i, down(a1), 2 + j] = (
                    wide(dwp[ch, i, down(a1), 2 + j]) + wide(r1[ch, i, 1, j])
                ).astype(BF16)
            send(tag + "2m", dwp.at[ch, i, down(a1)], r2.at[ch, i, 1], m1)

    def reduce_3(ch):
        for i, (tag, a1, a2, p1, m1, p2, m2) in enumerate(halves):
            tag += str(ch)
            arrived(tag + "2p", r2.at[ch, i, 0])
            arrived(tag + "2m", r2.at[ch, i, 1])
            for j in range(4):
                st[ch, i, j] = (
                    wide(dwp[ch, i, a1, j]) + wide(r2[ch, i, 0, j]) + wide(r2[ch, i, 1, j])
                ).astype(BF16)
            send(tag + "3p", st.at[ch, i, across(a2), pl.ds(0, 32)], r3.at[ch, i, 0], p2)
            send(tag + "3m", st.at[ch, i, across(a2), pl.ds(32, 32)], r3.at[ch, i, 1], m2)

    def reduce_4(ch):
        for i, (tag, a1, a2, p1, m1, p2, m2) in enumerate(halves):
            tag += str(ch)
            arrived(tag + "3p", r3.at[ch, i, 0])
            st[ch, i, up(a2), 0:32] = (wide(st[ch, i, up(a2), 0:32]) + wide(r3[ch, i, 0])).astype(BF16)
            send(tag + "4p", st.at[ch, i, up(a2)], r4.at[ch, i, 0], p2)
            arrived(tag + "3m", r3.at[ch, i, 1])
            st[ch, i, down(a2), 32:64] = (
                wide(st[ch, i, down(a2), 32:64]) + wide(r3[ch, i, 1])
            ).astype(BF16)
            send(tag + "4m", st.at[ch, i, down(a2)], r4.at[ch, i, 1], m2)

    def update(ch):
        for i, (tag, a1, a2, p1, m1, p2, m2) in enumerate(halves):
            tag += str(ch)
            arrived(tag + "4p", r4.at[ch, i, 0])
            arrived(tag + "4m", r4.at[ch, i, 1])
            rows = slice(128 * i + 64 * ch, 128 * i + 64 * ch + 64)
            grad = (wide(st[ch, i, a2]) + wide(r4[ch, i, 0]) + wide(r4[ch, i, 1])) * scale
            new_moment = first_beta * mo[rows, :] + (1.0 - first_beta) * grad
            new_second = second_beta * se[rows, :] + (1.0 - second_beta) * grad * grad
            ratio = new_moment / first_fix / (jnp.sqrt(new_second / second_fix) + adam_eps)
            old = ma[rows, :]
            new_master = old - learn_rate * (ratio + weight_decay * old)
            mo[rows, :] = new_moment
            se[rows, :] = new_second
            ma[rows, :] = new_master
            nwb[i, ch] = new_master.astype(BF16)
        both = pl.ds(0, 2)
        send("nw" + str(ch), nwb.at[both, ch], nw_hbm.at[d, both, ch], intra)

    start_x(0)
    in_g.wait()
    in_w.wait()
    relay_b(0)
    start_x(1)
    arrived("G1", g2s.at[d])
    arrived("W", wsib)
    act_half(d)
    arrived("G0", g2.at[od])
    send("G2", g2.at[od], g2s.at[od], sibling)
    arrived("G2", g2s.at[od])
    act_half(od)
    relay_a(0)
    relay_b(1)

    send("Pd1", pbuf.at[d, 2 * oh + oc], arel.at[1], inter)
    send("Pd0", pbuf.at[d, 2 * oh + c], arel.at[0], intra)
    send("Pb0", pbuf.at[od, 2 * h + c], actr.at[me], intra)
    send("Pb1", pbuf.at[od, 2 * h + oc], actr.at[me], intra_o)
    send("Pa", pbuf.at[d, 2 * h + oc], actr.at[me], sibling)

    def pass_all(ch):
        pass_on("Xd", ch, x2t.at[slot(od, oh, c), ch])
        pass_on("Xc", ch, x2t.at[slot(od, h, c), ch])
        pass_on("Xa2", ch, x2t.at[slot(d, oh, c), ch, first])
        pass_on("Xb2", ch, x2t.at[slot(d, oh, c), ch, second])

    def all_passed(ch):
        arrived("Xe" + str(ch), x2t.at[slot(d, h, oc), ch])
        passed("Xd", ch, x2t.at[slot(od, oh, oc), ch])
        passed("Xc", ch, x2t.at[slot(od, h, oc), ch])
        passed("Xa2", ch, x2t.at[slot(d, oh, oc), ch, first])
        passed("Xb2", ch, x2t.at[slot(d, oh, oc), ch, second])

    pass_all(0)
    own_x.wait()
    all_passed(0)

    grad_tile(0, across(z), across(y))
    reduce_1(0)
    grad_tile(0, up(z), up(y))
    relay_a(1)
    send("Pc0", pbuf.at[od, 2 * oh + c], actr.at[me], inter)
    send("Pc1", pbuf.at[od, 2 * oh + oc], actr.at[me], inter_o)
    grad_tile(0, down(z), down(y))
    grad_tile(0, z, y)
    reduce_2(0)
    arrived("Pd1", arel.at[1])
    send("Pf1", arel.at[1], actr.at[slot(od, oh, c)], intra_o)

    pass_all(1)
    all_passed(1)
    grad_tile(1, across(z), across(y))
    reduce_1(1)
    reduce_3(0)
    grad_tile(1, up(z), up(y))
    grad_tile(1, down(z), down(y))
    reduce_4(0)
    grad_tile(1, z, y)
    reduce_2(1)
    arrived("Pd0", arel.at[0])
    send("Pf0", arel.at[0], actr.at[slot(od, h, c)], inter)
    in_ma.wait()
    in_mo.wait()
    in_se.wait()
    update(0)
    reduce_3(1)
    reduce_4(1)
    update(1)
    outs = [
        local("onw", nwb, nw_hbm.at[d]),
        local("onm", ma, nm_hbm),
        local("onmo", mo, nmo_hbm),
        local("ons", se, ns_hbm),
    ]

    arrived("Pa", actr.at[slot(d, h, oc)])
    arrived("Pb0", actr.at[slot(od, h, c)])
    arrived("Pb1", actr.at[slot(od, h, oc)])
    arrived("Pc0", actr.at[slot(od, oh, c)])
    arrived("Pc1", actr.at[slot(od, oh, oc)])
    arrived("Pf0", actr.at[slot(d, oh, c)])
    arrived("Pf1", actr.at[slot(d, oh, oc)])
    actr[me] = pbuf[d, m]
    for p in range(4):
        k = 4 * (p // 2) + p % 2
        both = wide(actr[k]) + wide(actr[k + 2])
        rbuf[p * 128:(p + 1) * 128, :] = both.astype(BF16)
        bsend[p:p + 1, :] = both[0:1]
    send("bnd", bsend, brecv, prev_dev)
    arrived("bnd", brecv)
    last = place == total - 1
    rows = lax.broadcasted_iota(jnp.int32, (512, 512), 0)
    cols = lax.broadcasted_iota(jnp.int32, (512, 512), 1)
    put = jnp.where(rows == 4 * (cols % 128) + cols // 128 - 3, 1.0, 0.0).astype(BF16)

    def finish(t, carry):
        span = pl.ds(pl.multiple_of(t * 512, 512), 512)
        out = jnp.dot(put, rbuf[:, span], preferred_element_type=F32)
        xf[0:496, span] = out[0:496].astype(BF16)
        tail = out[496:512]
        line = lax.broadcasted_iota(jnp.int32, (16, 512), 0)
        for p in range(3):
            row = jnp.where(last, 0.0, brecv[p:p + 1, span])
            tail = jnp.where(line == 13 + p, row, tail)
        xf[496:512, span] = tail.astype(BF16)
        return carry

    lax.fori_loop(0, 4, finish, 0)
    outs.append(local("oact", xf, act_hbm))
    for ch in range(2):
        arrived("nw" + str(ch), nw_hbm.at[od, pl.ds(0, 2), ch])
    for copy in outs:
        copy.wait()
    for copy in sent:
        copy.wait_send()


def per_device(shortening_input, coarse_grad, weight_copy, master, moment, second):
    x = shortening_input[0]
    g = coarse_grad[0]
    fine, features = x.shape
    width = g.shape[1]
    w = weight_copy.reshape(2, features, width)
    rows = master.shape[1]
    scale = 1.0 / math.sqrt(lax.axis_size("dp") * lax.axis_size("seq") * g.shape[0])
    any_spec = pl.BlockSpec(memory_space=pl.ANY)
    vm = pltpu.VMEM
    act, new_master, new_moment, new_second, new_weight = pl.pallas_call(
        functools.partial(kernel, scale),
        out_shape=(
            jax.ShapeDtypeStruct((fine, features), BF16),
            jax.ShapeDtypeStruct((rows, width), F32),
            jax.ShapeDtypeStruct((rows, width), F32),
            jax.ShapeDtypeStruct((rows, width), F32),
            jax.ShapeDtypeStruct((2, 2, 2, rows // 4, width), BF16),
        ),
        in_specs=[any_spec] * 6,
        out_specs=[any_spec] * 5,
        scratch_shapes=[
            vm((512, 2048), BF16),
            vm((2, 2, 32, 64, 128), BF16),
            vm((8, 2, 32, 64, 128), BF16),
            vm((2, 2, 16, 64, 128), BF16),
            vm((2, 512, 1024), BF16),
            vm((2, 512, 1024), BF16),
            vm((2048, 1024), BF16),
            vm((2048, 1024), BF16),
            vm((2, 4, 128, 2048), BF16),
            vm((8, 128, 2048), BF16),
            vm((2, 128, 2048), BF16),
            vm((512, 2048), BF16),
            vm((2, 2, 4, 4, 64, 1024), BF16),
            vm((2, 2, 2, 2, 64, 1024), BF16),
            vm((2, 2, 2, 4, 64, 1024), BF16),
            vm((2, 2, 4, 64, 1024), BF16),
            vm((2, 2, 2, 32, 1024), BF16),
            vm((2, 2, 2, 64, 1024), BF16),
            vm((256, 1024), F32),
            vm((256, 1024), F32),
            vm((256, 1024), F32),
            vm((2, 2, 64, 1024), BF16),
            vm((4, 2048), F32),
            vm((4, 2048), F32),
            pltpu.SemaphoreType.DMA((COPIES,)),
            pltpu.SemaphoreType.DMA((COPIES,)),
            pltpu.SemaphoreType.DMA((LOCALS,)),
        ],
        compiler_params=pltpu.CompilerParams(
            collective_id=0, has_side_effects=True, vmem_limit_bytes=66_000_000
        ),
    )(x, g, w, master[0], moment[0], second[0])
    return (act[None], new_master[None], new_moment[None], new_second[None], new_weight.reshape(2, rows, width))


def solution(mesh):
    return jax.shard_map(
        per_device,
        mesh=mesh,
        in_specs=(
            P("dp", ("seq", "mp"), None),
            P("dp", "seq", "mp"),
            P("dp", None, "mp"),
            P("dp", "seq", "mp"),
            P("dp", "seq", "mp"),
            P("dp", "seq", "mp"),
        ),
        out_specs=(
            P("dp", ("seq", "mp"), None),
            P("dp", "seq", "mp"),
            P("dp", "seq", "mp"),
            P("dp", "seq", "mp"),
            P(None, "seq", "mp"),
        ),
        check_vma=False,
    )
```

time: 599 us -> 146 us (0.24)
  waiting for transfers between devices: 508 us -> 0 us
  Pallas kernels: 0 us -> 138 us
  matrix products: 47.4 us -> 0 us
  local copies, waits for them, and re-layouts: 21.2 us -> 7.77 us
  between operations: 13.8 us -> 0.65 us
    reduce_scatter x2 -> x0, waiting for transfers between devices: 253 us -> none  [the longest x1 161 us: per_device(): lax.psum_scatter(lax.dot_general(gathered, grad_cols, (((0,), (0,)), ((),...]
    all_gather x3 -> x0, waiting for transfers between devices: 250 us -> none  [the longest x1 169 us: per_device(): whole_copy = lax.all_gather(weight_copy, 'dp', axis=0, tiled=True)]
    pallas_call x0 -> x1, Pallas kernels: none -> 138 us  [per_device(): pl.pallas_call(functools.partial(kernel, scale), out_shape=(jax.ShapeDtyp...]
    dot_general x2 -> x0, matrix products: 47.4 us -> none  [the longest x1 29.6 us: per_device(): lax.dot_general(grad_cols, weights, (((1,), (1,)), ((), ())), preferred_e...]
    reshape x2 -> x0, local copies, waits for them, and re-layouts: 18.4 us -> none  [the longest x1 15.1 us: per_device(): lax.all_gather(fine_rows, 'mp', axis=0, tiled=True)]
  transfers between devices with their start and end apart: 6 -> 0, of which waited for: 6 -> 0; matrix products, arithmetic and copies ran while one was open for 12% -> 0% of each run, Pallas kernels for 0% -> 0%
where the time goes in v1:
time: 146 us
  Pallas kernels  138 us (95%)
  local copies, waits for them, and re-layouts  7.77 us (5%)
    pallas_call x1, Pallas kernels, per_device(): pl.pallas_call(functools.partial(kernel, scale), out_shape=(jax.ShapeDtyp...  138 us
    unnamed x13, local copies, waits for them, and re-layouts  7.77 us

profile of v1, /device:TPU:1, one launch (start us, length us, event | category | flops | bytes accessed | tf_op | source)
XLA Modules:
  0.0 146.0 jit_solution(4596609549548827467)
XLA Ops:
  0.6 137.6 %shard_map.101 = (bf16[512,2048]{1,0:T(8,128)(2,1)}, f32[256,1024]{1,0:T(8,128)}, f32[256,1024]{1,0:T(8,128)}, f32[256,1024]{1,0:T(8,128)}, bf16[2,2,2,64,1024]{4,3,2,1,0:T(8,128)(2,1)}) custom-call(bf16[512,2048]{1,0:T(8,128)(2,1)} %bitcast.12, bf16[512,1024]{1,0:T(8,128)(2,1)} %bitcast.14, bf16[2,2048,1024]{2,1,0:T(8,128)(2,1)} %bitcast.11, ...), custom_call_target="tpu_custom_call" | custom-call | tf_op jit(solution)/shard_map/pallas_call | solution.py:380
  138.2 0.0 copy-start.3
  138.2 3.2 %copy.16 = bf16[1,512,2048]{2,1,0:T(8,128)(2,1)} copy(bf16[1,512,2048]{2,1,0:T(8,128)(2,1)} %bitcast.13) | data formatting | bytes 4194304
  141.4 0.0 copy-done.3
  141.5 0.0 copy-start.2
  141.5 0.0 copy-start.1
  141.5 1.0 copy.17
  142.4 0.6 copy-done.2
  143.1 0.0 copy-start
  143.1 1.0 copy.18
  144.0 0.0 copy-done.1
  144.0 1.0 copy.19
  145.0 0.0 copy-done
  145.0 1.0 copy.20
Async XLA Ops:
  138.2 3.3 %copy-start.3 = (f32[256,1024]{1,0:T(8,128)S(1)}, f32[256,1024]{1,0:T(8,128)}, u32[]{:S(2)}) copy-start(f32[256,1024]{1,0:T(8,128)} %get-tuple-element.11) | copy-start | bytes 3145732
  141.5 1.6 %copy-start.2 = (f32[256,1024]{1,0:T(8,128)S(1)}, f32[256,1024]{1,0:T(8,128)}, u32[]{:S(2)}) copy-start(f32[256,1024]{1,0:T(8,128)} %get-tuple-element.12) | copy-start | bytes 3145732
  141.5 2.6 %copy-start.1 = (f32[256,1024]{1,0:T(8,128)S(1)}, f32[256,1024]{1,0:T(8,128)}, u32[]{:S(2)}) copy-start(f32[256,1024]{1,0:T(8,128)} %get-tuple-element.13) | copy-start | bytes 3145732
  143.1 1.9 %copy-start = (bf16[2,2,2,64,1024]{4,3,2,1,0:T(8,128)(2,1)S(1)}, bf16[2,2,2,64,1024]{4,3,2,1,0:T(8,128)(2,1)}, u32[]{:S(2)}) copy-start(bf16[2,2,2,64,1024]{4,3,2,1,0:T(8,128)(2,1)} %get-tuple-element.14) | copy-start | bytes 3145732

commit v2 on v1

--- a/solution.py
+++ b/solution.py
@@ -29,9 +29,9 @@
 
 def kernel(
     scale, x_hbm, g_hbm, w_hbm, ma_hbm, mo_hbm, se_hbm,
-    act_hbm, nm_hbm, nmo_hbm, ns_hbm, nw_hbm,
-    xf, xall, x2t, xrel, g2, g2s, wown, wsib, pbuf, actr, arel, rbuf,
-    dwp, r1, r2, st, r3, r4, ma, mo, se, nwb, bsend, brecv,
+    rbuf, brecv, ma, mo, se, nw,
+    xf, xall, x2t, xrel, g2, g2s, wown, wsib, pbuf, actr, arel,
+    dwp, r1, r2, st, r3, r4, bsend,
     send_sem, recv_sem, local_sem,
 ):
     d = lax.axis_index("dp")
@@ -245,9 +245,9 @@
             mo[rows, :] = new_moment
             se[rows, :] = new_second
             ma[rows, :] = new_master
-            nwb[i, ch] = new_master.astype(BF16)
+            nw[d, i, ch] = new_master.astype(BF16)
         both = pl.ds(0, 2)
-        send("nw" + str(ch), nwb.at[both, ch], nw_hbm.at[d, both, ch], intra)
+        send("nw" + str(ch), nw.at[d, both, ch], nw.at[d, both, ch], intra)
 
     start_x(0)
     in_g.wait()
@@ -318,13 +318,6 @@
     reduce_3(1)
     reduce_4(1)
     update(1)
-    outs = [
-        local("onw", nwb, nw_hbm.at[d]),
-        local("onm", ma, nm_hbm),
-        local("onmo", mo, nmo_hbm),
-        local("ons", se, ns_hbm),
-    ]
-
     arrived("Pa", actr.at[slot(d, h, oc)])
     arrived("Pb0", actr.at[slot(od, h, c)])
     arrived("Pb1", actr.at[slot(od, h, oc)])
@@ -340,31 +333,38 @@
         bsend[p:p + 1, :] = both[0:1]
     send("bnd", bsend, brecv, prev_dev)
     arrived("bnd", brecv)
-    last = place == total - 1
+    for ch in range(2):
+        arrived("nw" + str(ch), nw.at[od, pl.ds(0, 2), ch])
+    for copy in sent:
+        copy.wait_send()
+
+
+def finish(r_ref, b_ref, ma, mo, se, nw, act_out, nm_out, nmo_out, ns_out, nw_out, act, act_sem, sem):
+    copies = [
+        pltpu.make_async_copy(src, dst, sem.at[i])
+        for i, (src, dst) in enumerate(((ma, nm_out), (mo, nmo_out), (se, ns_out), (nw, nw_out)))
+    ]
+    for copy in copies:
+        copy.start()
+    last = lax.axis_index("seq") * 4 + lax.axis_index("mp") == 63
     rows = lax.broadcasted_iota(jnp.int32, (512, 512), 0)
     cols = lax.broadcasted_iota(jnp.int32, (512, 512), 1)
     put = jnp.where(rows == 4 * (cols % 128) + cols // 128 - 3, 1.0, 0.0).astype(BF16)
-
-    def finish(t, carry):
-        span = pl.ds(pl.multiple_of(t * 512, 512), 512)
-        out = jnp.dot(put, rbuf[:, span], preferred_element_type=F32)
-        xf[0:496, span] = out[0:496].astype(BF16)
+    line = lax.broadcasted_iota(jnp.int32, (16, 512), 0)
+    for t in range(4):
+        span = pl.ds(t * 512, 512)
+        out = jnp.dot(put, r_ref[:, span], preferred_element_type=F32)
+        act[0:496, span] = out[0:496].astype(BF16)
         tail = out[496:512]
-        line = lax.broadcasted_iota(jnp.int32, (16, 512), 0)
         for p in range(3):
-            row = jnp.where(last, 0.0, brecv[p:p + 1, span])
+            row = jnp.where(last, 0.0, b_ref[p:p + 1, span])
             tail = jnp.where(line == 13 + p, row, tail)
-        xf[496:512, span] = tail.astype(BF16)
-        return carry
-
-    lax.fori_loop(0, 4, finish, 0)
-    outs.append(local("oact", xf, act_hbm))
-    for ch in range(2):
-        arrived("nw" + str(ch), nw_hbm.at[od, pl.ds(0, 2), ch])
-    for copy in outs:
+        act[496:512, span] = tail.astype(BF16)
+        copy = pltpu.make_async_copy(act.at[:, span], act_out.at[:, span], act_sem.at[t])
+        copy.start()
+        copies.append(copy)
+    for copy in copies:
         copy.wait()
-    for copy in sent:
-        copy.wait_send()
 
 
 def per_device(shortening_input, coarse_grad, weight_copy, master, moment, second):
@@ -377,17 +377,18 @@
     scale = 1.0 / math.sqrt(lax.axis_size("dp") * lax.axis_size("seq") * g.shape[0])
     any_spec = pl.BlockSpec(memory_space=pl.ANY)
     vm = pltpu.VMEM
-    act, new_master, new_moment, new_second, new_weight = pl.pallas_call(
+    held = pl.pallas_call(
         functools.partial(kernel, scale),
         out_shape=(
-            jax.ShapeDtypeStruct((fine, features), BF16),
-            jax.ShapeDtypeStruct((rows, width), F32),
-            jax.ShapeDtypeStruct((rows, width), F32),
-            jax.ShapeDtypeStruct((rows, width), F32),
-            jax.ShapeDtypeStruct((2, 2, 2, rows // 4, width), BF16),
+            vm((fine, features), BF16),
+            vm((4, features), F32),
+            vm((rows, width), F32),
+            vm((rows, width), F32),
+            vm((rows, width), F32),
+            vm((2, 2, 2, rows // 4, width), BF16),
         ),
         in_specs=[any_spec] * 6,
-        out_specs=[any_spec] * 5,
+        out_specs=[pl.BlockSpec(memory_space=pltpu.VMEM)] * 6,
         scratch_shapes=[
             vm((512, 2048), BF16),
             vm((2, 2, 32, 64, 128), BF16),
@@ -400,27 +401,39 @@
             vm((2, 4, 128, 2048), BF16),
             vm((8, 128, 2048), BF16),
             vm((2, 128, 2048), BF16),
-            vm((512, 2048), BF16),
             vm((2, 2, 4, 4, 64, 1024), BF16),
             vm((2, 2, 2, 2, 64, 1024), BF16),
             vm((2, 2, 2, 4, 64, 1024), BF16),
             vm((2, 2, 4, 64, 1024), BF16),
             vm((2, 2, 2, 32, 1024), BF16),
             vm((2, 2, 2, 64, 1024), BF16),
-            vm((256, 1024), F32),
-            vm((256, 1024), F32),
-            vm((256, 1024), F32),
-            vm((2, 2, 64, 1024), BF16),
-            vm((4, 2048), F32),
             vm((4, 2048), F32),
             pltpu.SemaphoreType.DMA((COPIES,)),
             pltpu.SemaphoreType.DMA((COPIES,)),
             pltpu.SemaphoreType.DMA((LOCALS,)),
         ],
         compiler_params=pltpu.CompilerParams(
-            collective_id=0, has_side_effects=True, vmem_limit_bytes=66_000_000
+            collective_id=0, has_side_effects=True, vmem_limit_bytes=57_500_000
         ),
     )(x, g, w, master[0], moment[0], second[0])
+    act, new_master, new_moment, new_second, new_weight = pl.pallas_call(
+        finish,
+        out_shape=(
+            jax.ShapeDtypeStruct((fine, features), BF16),
+            jax.ShapeDtypeStruct((rows, width), F32),
+            jax.ShapeDtypeStruct((rows, width), F32),
+            jax.ShapeDtypeStruct((rows, width), F32),
+            jax.ShapeDtypeStruct((2, 2, 2, rows // 4, width), BF16),
+        ),
+        in_specs=[pl.BlockSpec(memory_space=pltpu.VMEM)] * 2 + [any_spec] * 4,
+        out_specs=[any_spec] * 5,
+        scratch_shapes=[
+            vm((fine, features), BF16),
+            pltpu.SemaphoreType.DMA((4,)),
+            pltpu.SemaphoreType.DMA((4,)),
+        ],
+        compiler_params=pltpu.CompilerParams(vmem_limit_bytes=16_000_000),
+    )(*held)
     return (act[None], new_master[None], new_moment[None], new_second[None], new_weight.reshape(2, rows, width))
 
 

time: 146 us -> 138 us (0.945)
  local copies, waits for them, and re-layouts: 7.77 us -> 0 us
    unnamed x13 -> x0, local copies, waits for them, and re-layouts: 7.77 us -> none
    pallas_call x1 -> x2, Pallas kernels: 138 us -> 137 us  [the longest x1 134 us: per_device(): pl.pallas_call(functools.partial(kernel, scale), out_shape=(vm((fine, fea...]
where the time goes in v2:
time: 138 us
  Pallas kernels  137 us (99%)
    pallas_call x1, Pallas kernels, per_device(): pl.pallas_call(functools.partial(kernel, scale), out_shape=(vm((fine, fea...  134 us
    pallas_call x1, Pallas kernels, per_device(): pl.pallas_call(finish, out_shape=(jax.ShapeDtypeStruct((fine, features),...  2.92 us

profile of v2, /device:TPU:1, one launch (start us, length us, event | category | flops | bytes accessed | tf_op | source)
XLA Modules:
  0.0 137.9 jit_solution(1882570175209979751)
XLA Ops:
  0.6 134.3 %shard_map.101 = (bf16[512,2048]{1,0:T(8,128)(2,1)S(1)}, f32[4,2048]{1,0:T(4,128)S(1)}, f32[256,1024]{1,0:T(8,128)S(1)}, f32[256,1024]{1,0:T(8,128)S(1)}, f32[25...) custom-call(bf16[512,2048]{1,0:T(8,128)(2,1)} %bitcast.12, bf16[512,1024]{1,0:T(8,128)(2,1)} %bitcast.13, ...), custom_call_target="tpu_custom_call" | custom-call | tf_op jit(solution)/shard_map/pallas_call | solution.py:380
  134.9 2.9 %shard_map.102 = (bf16[512,2048]{1,0:T(8,128)(2,1)}, f32[256,1024]{1,0:T(8,128)}, f32[256,1024]{1,0:T(8,128)}, f32[256,1024]{1,0:T(8,128)}, bf16[2,2,2,64,1024]{4,3,2,1,0:T(8,128)(2,1)}) custom-call(bf16[512,2048]{1,0:T(8,128)(2,1)S(1)} %get-tuple-element.16.r_ref, f32[4,2048]{1,0:T(4,128)S(1)} %get-tuple-element.17.b_ref, ...), custom_call_target="tpu_custom_call" | custom-call | tf_op jit(solution)/shard_map/pallas_call | solution.py:419

commit v3 on v2

--- a/solution.py
+++ b/solution.py
@@ -20,7 +20,8 @@
 learn_rate = 0.05
 weight_decay = 0.1
 
-COPIES = 80
+COPIES = 96
+OWNED = 92
 LOCALS = 16
 
 F32 = jnp.float32
@@ -30,8 +31,8 @@
 def kernel(
     scale, x_hbm, g_hbm, w_hbm, ma_hbm, mo_hbm, se_hbm,
     rbuf, brecv, ma, mo, se, nw,
-    xf, xall, x2t, xrel, g2, g2s, wown, wsib, pbuf, actr, arel,
-    dwp, r1, r2, st, r3, r4, bsend,
+    xf, xall, x2t, xrel, gall, wown, wsib, pbuf, actr, arel,
+    dwp, r1, r2, st, r3, r4, rsend, gr, bsend,
     send_sem, recv_sem, local_sem,
 ):
     d = lax.axis_index("dp")
@@ -67,7 +68,7 @@
     prev_dev = {"seq": before // 4, "mp": before % 4}
     next_dev = {"seq": after // 4, "mp": after % 4}
 
-    sent, ids, local_ids = [], {}, {}
+    sent, maybe, ids, local_ids = [], [], {}, {}
 
     def send(name, src, dst, device):
         i = ids.setdefault(name, len(ids))
@@ -91,7 +92,7 @@
         return copy
 
     in_x = local("x", x_hbm, xf)
-    in_g = local("g", g_hbm, g2.at[d])
+    in_g = local("g", g_hbm, gall.at[me])
     in_w = local("w", w_hbm.at[c], wown)
     in_ma = local("ma", ma_hbm, ma)
     in_mo = local("mo", mo_hbm, mo)
@@ -101,10 +102,22 @@
     partners = (sibling, intra, intra_o, inter, inter_o, zp, zm, yp, ym, prev_dev, next_dev)
     for device in partners:
         pl.semaphore_signal(barrier, inc=1, device_id=device, device_id_type=MESH)
-    pl.semaphore_wait(barrier, len(partners))
-
-    send("G0", g_hbm, g2.at[d], intra)
-    send("G1", g_hbm, g2s.at[d], sibling)
+    alone = z == m
+
+    def owner_device(j):
+        return {"seq": m * SIDE + y, "mp": j}
+
+    def source_device(j):
+        return {"seq": j * SIDE + y, "mp": z}
+
+    for j in range(SIDE):
+        for device in (owner_device(j), source_device(j)):
+            pl.semaphore_signal(barrier, inc=1, device_id=device, device_id_type=MESH)
+    pl.semaphore_wait(barrier, len(partners) + 2 * SIDE)
+
+    send("Gi", g_hbm, gall.at[me], intra)
+    send("Gx", g_hbm, gall.at[me], inter)
+    send("Gs", g_hbm, gall.at[me], sibling)
     send("W", w_hbm.at[oc], wsib, sibling)
 
     in_x.wait()
@@ -117,66 +130,47 @@
         got = jnp.dot(pick, xf[:, pl.ds(pl.multiple_of(tile * 512, 512), 512)], preferred_element_type=F32)
         turned = got.T.astype(BF16)
         for j in range(4):
-            owner = (p % 2) * 8 + tile * 2 + j // 2
-            where = owner if j % 2 == 0 else 16 + (owner % SIDE) * SIDE + owner // SIDE
-            for ch in range(2):
-                xall[p // 2, ch, where] = turned[j * 128 + ch * 64:j * 128 + ch * 64 + 64]
+            block = turned[j * 128:(j + 1) * 128].reshape(2, 64, 128)
+            xall[p * 2 + tile // 2, (tile % 2) * 2 + j // 2, pl.ds((j % 2) * 2, 2)] = block
         return carry
 
     lax.fori_loop(0, 16, turn, 0)
-    own_x = local("xown", xall.at[d], x2t.at[me])
-    first, second = pl.ds(0, 16), pl.ds(16, 16)
-
-    def start_x(ch):
-        tag = str(ch)
-        send("Xa" + tag, xall.at[d, ch, first], xrel.at[ch, 0], intra)
-        send("Xb" + tag, xall.at[d, ch, second], xrel.at[ch, 1], inter)
-        send("Xd" + tag, xall.at[od, ch], x2t.at[me, ch], inter)
-        send("Xc" + tag, xall.at[od, ch], x2t.at[me, ch], intra)
-        send("Xe" + tag, xall.at[d, ch], x2t.at[me, ch], sibling)
-
-    def relay_b(ch):
-        arrived("Xb" + str(ch), xrel.at[ch, 1])
-        send("Xb2" + str(ch), xrel.at[ch, 1], x2t.at[slot(od, oh, c), ch, second], intra)
-
-    def relay_a(ch):
-        arrived("Xa" + str(ch), xrel.at[ch, 0])
-        send("Xa2" + str(ch), xrel.at[ch, 0], x2t.at[slot(od, h, c), ch, first], inter)
-
-    def pass_on(name, ch, dst):
-        arrived(name + str(ch), dst)
-        send("F" + name + str(ch), dst, dst, sibling)
-
-    def passed(name, ch, dst):
-        arrived("F" + name + str(ch), dst)
+    own_x = local("xown", xall.at[me], x2t.at[me])
+    send("Xa", xall.at[slot(d, oh, c)], xrel.at[0], intra)
+    send("Xb", xall.at[slot(d, oh, oc)], xrel.at[1], inter)
+    send("Xi0", xall.at[slot(od, h, c)], x2t.at[me], intra)
+    send("Xi1", xall.at[slot(od, h, oc)], x2t.at[me], intra_o)
+    send("Xx0", xall.at[slot(od, oh, c)], x2t.at[me], inter)
+    send("Xx1", xall.at[slot(od, oh, oc)], x2t.at[me], inter_o)
+    send("Xs", xall.at[slot(d, h, oc)], x2t.at[me], sibling)
 
     def act_half(dd):
         def step(t, carry):
             outs = pl.ds(pl.multiple_of(t * 256, 256), 256)
             dims = (((1,), (1,)), ((), ()))
-            part = lax.dot_general(g2[dd], wown[outs, :], dims, preferred_element_type=F32)
-            part += lax.dot_general(g2s[dd], wsib[outs, :], dims, preferred_element_type=F32)
+            part = lax.dot_general(gall[4 * dd + m], wown[outs, :], dims, preferred_element_type=F32)
+            part += lax.dot_general(gall[4 * dd + 2 * h + oc], wsib[outs, :], dims, preferred_element_type=F32)
             pbuf[dd, :, :, outs] = part.astype(BF16).reshape(4, 128, 256)
             return carry
 
         lax.fori_loop(0, 8, step, 0)
 
     def grad_tile(ch, group_a, group_b):
-        tile_a, tile_b = pl.ds(4 * group_a, 4), pl.ds(16 + 4 * group_b, 4)
+        side = h if ch == 0 else oh
 
         def step(t, carry):
             cols = pl.ds(pl.multiple_of(t * 256, 256), 256)
-            left = jnp.concatenate(
-                [
-                    jnp.concatenate([x2t[k, ch, tile].reshape(256, 128) for k in range(8)], axis=1)
-                    for tile in (tile_a, tile_b)
-                ],
-                axis=0,
-            )
-            right = jnp.concatenate([g2[0, :, cols], g2[1, :, cols]], axis=0)
-            part = jnp.dot(left, right, preferred_element_type=F32).astype(BF16).reshape(2, 4, 64, 256)
-            dwp[ch, 0, group_a, :, :, cols] = part[0]
-            dwp[ch, 1, group_b, :, :, cols] = part[1]
+
+            def product(rows, column):
+                left = jnp.concatenate([rows(k).reshape(256, 128) for k in range(8)], axis=1)
+                right = jnp.concatenate(
+                    [gall[2 * side + column, :, cols], gall[4 + 2 * side + column, :, cols]], axis=0
+                )
+                part = jnp.dot(left, right, preferred_element_type=F32)
+                return part.astype(BF16).reshape(4, 64, 256)
+
+            dwp[ch, 0, group_a, :, :, cols] = product(lambda k: x2t[k, :, group_a], 0)
+            dwp[ch, 1, group_b, :, :, cols] = product(lambda k: x2t[k, group_b], 1)
             return carry
 
         lax.fori_loop(0, 4, step, 0)
@@ -230,13 +224,41 @@
             ).astype(BF16)
             send(tag + "4m", st.at[ch, i, down(a2)], r4.at[ch, i, 1], m2)
 
-    def update(ch):
+    def hand_over(ch):
         for i, (tag, a1, a2, p1, m1, p2, m2) in enumerate(halves):
             tag += str(ch)
             arrived(tag + "4p", r4.at[ch, i, 0])
             arrived(tag + "4m", r4.at[ch, i, 1])
-            rows = slice(128 * i + 64 * ch, 128 * i + 64 * ch + 64)
-            grad = (wide(st[ch, i, a2]) + wide(r4[ch, i, 0]) + wide(r4[ch, i, 1])) * scale
+            rsend[ch, i] = (wide(st[ch, i, a2]) + wide(r4[ch, i, 0]) + wide(r4[ch, i, 1])).astype(BF16)
+            column = 2 * (h if ch == 0 else oh) + i
+            k = ids.setdefault("R" + tag, len(ids))
+            copy = pltpu.make_async_remote_copy(
+                src_ref=rsend.at[ch, i], dst_ref=gr.at[z], send_sem=send_sem.at[k], recv_sem=recv_sem.at[OWNED + z],
+                device_id=owner_device(column), device_id_type=MESH,
+            )
+            if ch == 1:
+                copy.start()
+                sent.append(copy)
+                continue
+            mine = alone & (c == i)
+            maybe.append((mine, copy))
+
+            @pl.when(jnp.logical_not(mine))
+            def _():
+                copy.start()
+
+            @pl.when(mine)
+            def _():
+                pltpu.make_async_copy(rsend.at[ch, i], gr.at[z], recv_sem.at[OWNED + z]).start()
+
+    def update():
+        for j in range(SIDE):
+            pltpu.make_async_remote_copy(
+                src_ref=gr.at[j], dst_ref=gr.at[j], send_sem=send_sem.at[OWNED + j], recv_sem=recv_sem.at[OWNED + j],
+                device_id=sibling, device_id_type=MESH,
+            ).wait_recv()
+            rows = slice(64 * j, 64 * j + 64)
+            grad = wide(gr[j]) * scale
             new_moment = first_beta * mo[rows, :] + (1.0 - first_beta) * grad
             new_second = second_beta * se[rows, :] + (1.0 - second_beta) * grad * grad
             ratio = new_moment / first_fix / (jnp.sqrt(new_second / second_fix) + adam_eps)
@@ -245,62 +267,60 @@
             mo[rows, :] = new_moment
             se[rows, :] = new_second
             ma[rows, :] = new_master
-            nw[d, i, ch] = new_master.astype(BF16)
-        both = pl.ds(0, 2)
-        send("nw" + str(ch), nw.at[d, both, ch], nw.at[d, both, ch], intra)
-
-    start_x(0)
+            nw[d, rows, :] = new_master.astype(BF16)
+            if j % 2 == 1:
+                both = pl.ds(64 * j - 64, 128)
+                send("nw" + str(j // 2), nw.at[d, both], nw.at[d, both], intra)
+
+    def pass_on(name, came, dst):
+        arrived(came, dst)
+        send(name, dst, dst, sibling)
+
     in_g.wait()
     in_w.wait()
-    relay_b(0)
-    start_x(1)
-    arrived("G1", g2s.at[d])
+    arrived("Gs", gall.at[slot(d, h, oc)])
     arrived("W", wsib)
     act_half(d)
-    arrived("G0", g2.at[od])
-    send("G2", g2.at[od], g2s.at[od], sibling)
-    arrived("G2", g2s.at[od])
+    pass_on("Fi", "Gi", gall.at[slot(od, h, c)])
+    pass_on("Fx", "Gx", gall.at[slot(od, oh, c)])
+    arrived("Xa", xrel.at[0])
+    send("Xa2", xrel.at[0], x2t.at[slot(od, h, c)], inter)
+    arrived("Xb", xrel.at[1])
+    send("Xb2", xrel.at[1], x2t.at[slot(od, oh, c)], intra_o)
+    most, rest = pl.ds(0, 384), pl.ds(384, 128)
+    send("Ga", gall.at[slot(od, h, c), most], gall.at[slot(od, h, c), most], inter)
+    send("Gb", gall.at[slot(od, oh, c), rest], gall.at[slot(od, oh, c), rest], intra)
+    arrived("Fi", gall.at[slot(od, h, oc)])
     act_half(od)
-    relay_a(0)
-    relay_b(1)
 
     send("Pd1", pbuf.at[d, 2 * oh + oc], arel.at[1], inter)
     send("Pd0", pbuf.at[d, 2 * oh + c], arel.at[0], intra)
     send("Pb0", pbuf.at[od, 2 * h + c], actr.at[me], intra)
     send("Pb1", pbuf.at[od, 2 * h + oc], actr.at[me], intra_o)
+    send("Pc0", pbuf.at[od, 2 * oh + c], actr.at[me], inter)
+    send("Pc1", pbuf.at[od, 2 * oh + oc], actr.at[me], inter_o)
     send("Pa", pbuf.at[d, 2 * h + oc], actr.at[me], sibling)
 
-    def pass_all(ch):
-        pass_on("Xd", ch, x2t.at[slot(od, oh, c), ch])
-        pass_on("Xc", ch, x2t.at[slot(od, h, c), ch])
-        pass_on("Xa2", ch, x2t.at[slot(d, oh, c), ch, first])
-        pass_on("Xb2", ch, x2t.at[slot(d, oh, c), ch, second])
-
-    def all_passed(ch):
-        arrived("Xe" + str(ch), x2t.at[slot(d, h, oc), ch])
-        passed("Xd", ch, x2t.at[slot(od, oh, oc), ch])
-        passed("Xc", ch, x2t.at[slot(od, h, oc), ch])
-        passed("Xa2", ch, x2t.at[slot(d, oh, oc), ch, first])
-        passed("Xb2", ch, x2t.at[slot(d, oh, oc), ch, second])
-
-    pass_all(0)
     own_x.wait()
-    all_passed(0)
+    arrived("Xs", x2t.at[slot(d, h, oc)])
+    arrived("Xi0", x2t.at[slot(od, h, c)])
+    arrived("Xi1", x2t.at[slot(od, h, oc)])
+    arrived("Xx0", x2t.at[slot(od, oh, c)])
+    arrived("Xx1", x2t.at[slot(od, oh, oc)])
+    arrived("Xa2", x2t.at[slot(d, oh, c)])
+    arrived("Xb2", x2t.at[slot(d, oh, oc)])
 
     grad_tile(0, across(z), across(y))
     reduce_1(0)
     grad_tile(0, up(z), up(y))
-    relay_a(1)
-    send("Pc0", pbuf.at[od, 2 * oh + c], actr.at[me], inter)
-    send("Pc1", pbuf.at[od, 2 * oh + oc], actr.at[me], inter_o)
     grad_tile(0, down(z), down(y))
+    pass_on("Fb", "Gb", gall.at[slot(d, oh, c), rest])
     grad_tile(0, z, y)
     reduce_2(0)
-    arrived("Pd1", arel.at[1])
-    send("Pf1", arel.at[1], actr.at[slot(od, oh, c)], intra_o)
-
-    pass_all(1)
-    all_passed(1)
+    pass_on("Fa", "Ga", gall.at[slot(d, oh, c), most])
+    arrived("Fx", gall.at[slot(od, oh, oc)])
+    arrived("Fb", gall.at[slot(d, oh, oc), rest])
+    arrived("Fa", gall.at[slot(d, oh, oc), most])
     grad_tile(1, across(z), across(y))
     reduce_1(1)
     reduce_3(0)
@@ -308,16 +328,20 @@
     grad_tile(1, down(z), down(y))
     reduce_4(0)
     grad_tile(1, z, y)
-    reduce_2(1)
     arrived("Pd0", arel.at[0])
     send("Pf0", arel.at[0], actr.at[slot(od, h, c)], inter)
+    reduce_2(1)
+    arrived("Pd1", arel.at[1])
+    send("Pf1", arel.at[1], actr.at[slot(od, oh, c)], intra_o)
+    hand_over(0)
     in_ma.wait()
     in_mo.wait()
     in_se.wait()
-    update(0)
     reduce_3(1)
     reduce_4(1)
-    update(1)
+    hand_over(1)
+    update()
+
     arrived("Pa", actr.at[slot(d, h, oc)])
     arrived("Pb0", actr.at[slot(od, h, c)])
     arrived("Pb1", actr.at[slot(od, h, oc)])
@@ -333,8 +357,14 @@
         bsend[p:p + 1, :] = both[0:1]
     send("bnd", bsend, brecv, prev_dev)
     arrived("bnd", brecv)
-    for ch in range(2):
-        arrived("nw" + str(ch), nw.at[od, pl.ds(0, 2), ch])
+    for j in range(2):
+        arrived("nw" + str(j), nw.at[od, pl.ds(128 * j, 128)])
+    for mine, copy in maybe:
+
+        @pl.when(jnp.logical_not(mine))
+        def _():
+            copy.wait_send()
+
     for copy in sent:
         copy.wait_send()
 
@@ -385,17 +415,16 @@
             vm((rows, width), F32),
             vm((rows, width), F32),
             vm((rows, width), F32),
-            vm((2, 2, 2, rows // 4, width), BF16),
+            vm((2, rows, width), BF16),
         ),
         in_specs=[any_spec] * 6,
         out_specs=[pl.BlockSpec(memory_space=pltpu.VMEM)] * 6,
         scratch_shapes=[
             vm((512, 2048), BF16),
-            vm((2, 2, 32, 64, 128), BF16),
-            vm((8, 2, 32, 64, 128), BF16),
-            vm((2, 2, 16, 64, 128), BF16),
-            vm((2, 512, 1024), BF16),
-            vm((2, 512, 1024), BF16),
+            vm((8, 4, 4, 64, 128), BF16),
+            vm((8, 4, 4, 64, 128), BF16),
+            vm((2, 4, 4, 64, 128), BF16),
+            vm((8, 512, 1024), BF16),
             vm((2048, 1024), BF16),
             vm((2048, 1024), BF16),
             vm((2, 4, 128, 2048), BF16),
@@ -407,6 +436,8 @@
             vm((2, 2, 4, 64, 1024), BF16),
             vm((2, 2, 2, 32, 1024), BF16),
             vm((2, 2, 2, 64, 1024), BF16),
+            vm((2, 2, 64, 1024), BF16),
+            vm((4, 64, 1024), BF16),
             vm((4, 2048), F32),
             pltpu.SemaphoreType.DMA((COPIES,)),
             pltpu.SemaphoreType.DMA((COPIES,)),
@@ -423,7 +454,7 @@
             jax.ShapeDtypeStruct((rows, width), F32),
             jax.ShapeDtypeStruct((rows, width), F32),
             jax.ShapeDtypeStruct((rows, width), F32),
-            jax.ShapeDtypeStruct((2, 2, 2, rows // 4, width), BF16),
+            jax.ShapeDtypeStruct((2, rows, width), BF16),
         ),
         in_specs=[pl.BlockSpec(memory_space=pltpu.VMEM)] * 2 + [any_spec] * 4,
         out_specs=[any_spec] * 5,
@@ -434,7 +465,7 @@
         ],
         compiler_params=pltpu.CompilerParams(vmem_limit_bytes=16_000_000),
     )(*held)
-    return (act[None], new_master[None], new_moment[None], new_second[None], new_weight.reshape(2, rows, width))
+    return (act[None], new_master[None], new_moment[None], new_second[None], new_weight)
 
 
 def solution(mesh):

time: 138 us -> 140 us (1.014)
  no operation moved by 1% of the time
where the time goes in v3:
time: 140 us; the launch traced here: 138 us
  Pallas kernels  138 us (99%)
    pallas_call x1, Pallas kernels, per_device(): pl.pallas_call(functools.partial(kernel, scale), out_shape=(vm((fine, fea...  135 us
    pallas_call x1, Pallas kernels, per_device(): pl.pallas_call(finish, out_shape=(jax.ShapeDtypeStruct((fine, features),...  2.92 us

profile of v3, /device:TPU:1, one launch (start us, length us, event | category | flops | bytes accessed | tf_op | source)
XLA Modules:
  0.0 138.5 jit_solution(6321863575902378370)
XLA Ops:
  0.6 134.9 %shard_map.101 = (bf16[512,2048]{1,0:T(8,128)(2,1)S(1)}, f32[4,2048]{1,0:T(4,128)S(1)}, f32[256,1024]{1,0:T(8,128)S(1)}, f32[256,1024]{1,0:T(8,128)S(1)}, f32[25...) custom-call(bf16[512,2048]{1,0:T(8,128)(2,1)} %bitcast.11, bf16[512,1024]{1,0:T(8,128)(2,1)} %bitcast.12, ...), custom_call_target="tpu_custom_call" | custom-call | tf_op jit(solution)/shard_map/pallas_call | solution.py:410
  135.6 2.9 %shard_map.102 = (bf16[512,2048]{1,0:T(8,128)(2,1)}, f32[256,1024]{1,0:T(8,128)}, f32[256,1024]{1,0:T(8,128)}, f32[256,1024]{1,0:T(8,128)}, bf16[2,256,1024]{2,1,0:T(8,128)(2,1)}) custom-call(bf16[512,2048]{1,0:T(8,128)(2,1)S(1)} %get-tuple-element.16.r_ref, f32[4,2048]{1,0:T(4,128)S(1)} %get-tuple-element.17.b_ref, f32[256,1024]{1,0:T(8,128)S(1)} %get-tuple-element.18.ma, ...), custom_call_target="tpu_custom_call" | custom-call | tf_op jit(solution)/shard_map/pallas_call | solution.py:450

commit v4 on v3

--- a/solution.py
+++ b/solution.py
@@ -20,8 +20,8 @@
 learn_rate = 0.05
 weight_decay = 0.1
 
-COPIES = 96
-OWNED = 92
+COPIES = 160
+OWNED = 152
 LOCALS = 16
 
 F32 = jnp.float32
@@ -115,8 +115,12 @@
             pl.semaphore_signal(barrier, inc=1, device_id=device, device_id_type=MESH)
     pl.semaphore_wait(barrier, len(partners) + 2 * SIDE)
 
-    send("Gi", g_hbm, gall.at[me], intra)
-    send("Gx", g_hbm, gall.at[me], inter)
+    span = (pl.ds(0, 512), pl.ds(512, 512))
+
+    def send_g(name, half, device):
+        send(name, g_hbm.at[:, span[half]], gall.at[me, :, span[half]], device)
+
+    send_g("Gi0", 0, intra)
     send("Gs", g_hbm, gall.at[me], sibling)
     send("W", w_hbm.at[oc], wsib, sibling)
 
@@ -136,15 +140,15 @@
 
     lax.fori_loop(0, 16, turn, 0)
     own_x = local("xown", xall.at[me], x2t.at[me])
+    send("Xb", xall.at[slot(d, oh, oc)], xrel.at[1], inter)
     send("Xa", xall.at[slot(d, oh, c)], xrel.at[0], intra)
-    send("Xb", xall.at[slot(d, oh, oc)], xrel.at[1], inter)
     send("Xi0", xall.at[slot(od, h, c)], x2t.at[me], intra)
     send("Xi1", xall.at[slot(od, h, oc)], x2t.at[me], intra_o)
     send("Xx0", xall.at[slot(od, oh, c)], x2t.at[me], inter)
     send("Xx1", xall.at[slot(od, oh, oc)], x2t.at[me], inter_o)
     send("Xs", xall.at[slot(d, h, oc)], x2t.at[me], sibling)
 
-    def act_half(dd):
+    def act_part(dd, start, stop):
         def step(t, carry):
             outs = pl.ds(pl.multiple_of(t * 256, 256), 256)
             dims = (((1,), (1,)), ((), ()))
@@ -153,18 +157,19 @@
             pbuf[dd, :, :, outs] = part.astype(BF16).reshape(4, 128, 256)
             return carry
 
-        lax.fori_loop(0, 8, step, 0)
+        lax.fori_loop(start, stop, step, 0)
 
     def grad_tile(ch, group_a, group_b):
-        side = h if ch == 0 else oh
+        side = h if ch < 2 else oh
 
         def step(t, carry):
             cols = pl.ds(pl.multiple_of(t * 256, 256), 256)
+            wide_cols = pl.ds(pl.multiple_of(ch % 2 * 512 + t * 256, 256), 256)
 
             def product(rows, column):
                 left = jnp.concatenate([rows(k).reshape(256, 128) for k in range(8)], axis=1)
                 right = jnp.concatenate(
-                    [gall[2 * side + column, :, cols], gall[4 + 2 * side + column, :, cols]], axis=0
+                    [gall[2 * side + column, :, wide_cols], gall[4 + 2 * side + column, :, wide_cols]], axis=0
                 )
                 part = jnp.dot(left, right, preferred_element_type=F32)
                 return part.astype(BF16).reshape(4, 64, 256)
@@ -173,7 +178,7 @@
             dwp[ch, 1, group_b, :, :, cols] = product(lambda k: x2t[k, group_b], 1)
             return carry
 
-        lax.fori_loop(0, 4, step, 0)
+        lax.fori_loop(0, 2, step, 0)
 
     def wide(v):
         return v.astype(F32)
@@ -230,13 +235,15 @@
             arrived(tag + "4p", r4.at[ch, i, 0])
             arrived(tag + "4m", r4.at[ch, i, 1])
             rsend[ch, i] = (wide(st[ch, i, a2]) + wide(r4[ch, i, 0]) + wide(r4[ch, i, 1])).astype(BF16)
-            column = 2 * (h if ch == 0 else oh) + i
+            column = 2 * (h if ch < 2 else oh) + i
+            mark = OWNED + 2 * z + ch % 2
+            home = gr.at[z, ch % 2]
             k = ids.setdefault("R" + tag, len(ids))
             copy = pltpu.make_async_remote_copy(
-                src_ref=rsend.at[ch, i], dst_ref=gr.at[z], send_sem=send_sem.at[k], recv_sem=recv_sem.at[OWNED + z],
+                src_ref=rsend.at[ch, i], dst_ref=home, send_sem=send_sem.at[k], recv_sem=recv_sem.at[mark],
                 device_id=owner_device(column), device_id_type=MESH,
             )
-            if ch == 1:
+            if ch >= 2:
                 copy.start()
                 sent.append(copy)
                 continue
@@ -249,25 +256,28 @@
 
             @pl.when(mine)
             def _():
-                pltpu.make_async_copy(rsend.at[ch, i], gr.at[z], recv_sem.at[OWNED + z]).start()
+                pltpu.make_async_copy(rsend.at[ch, i], home, recv_sem.at[mark]).start()
 
     def update():
         for j in range(SIDE):
-            pltpu.make_async_remote_copy(
-                src_ref=gr.at[j], dst_ref=gr.at[j], send_sem=send_sem.at[OWNED + j], recv_sem=recv_sem.at[OWNED + j],
-                device_id=sibling, device_id_type=MESH,
-            ).wait_recv()
             rows = slice(64 * j, 64 * j + 64)
-            grad = wide(gr[j]) * scale
-            new_moment = first_beta * mo[rows, :] + (1.0 - first_beta) * grad
-            new_second = second_beta * se[rows, :] + (1.0 - second_beta) * grad * grad
-            ratio = new_moment / first_fix / (jnp.sqrt(new_second / second_fix) + adam_eps)
-            old = ma[rows, :]
-            new_master = old - learn_rate * (ratio + weight_decay * old)
-            mo[rows, :] = new_moment
-            se[rows, :] = new_second
-            ma[rows, :] = new_master
-            nw[d, rows, :] = new_master.astype(BF16)
+            for half in range(2):
+                mark = OWNED + 2 * j + half
+                pltpu.make_async_remote_copy(
+                    src_ref=gr.at[j, half], dst_ref=gr.at[j, half], send_sem=send_sem.at[mark],
+                    recv_sem=recv_sem.at[mark], device_id=sibling, device_id_type=MESH,
+                ).wait_recv()
+                cols = slice(512 * half, 512 * half + 512)
+                grad = wide(gr[j, half]) * scale
+                new_moment = first_beta * mo[rows, cols] + (1.0 - first_beta) * grad
+                new_second = second_beta * se[rows, cols] + (1.0 - second_beta) * grad * grad
+                ratio = new_moment / first_fix / (jnp.sqrt(new_second / second_fix) + adam_eps)
+                old = ma[rows, cols]
+                new_master = old - learn_rate * (ratio + weight_decay * old)
+                mo[rows, cols] = new_moment
+                se[rows, cols] = new_second
+                ma[rows, cols] = new_master
+                nw[d, rows, cols] = new_master.astype(BF16)
             if j % 2 == 1:
                 both = pl.ds(64 * j - 64, 128)
                 send("nw" + str(j // 2), nw.at[d, both], nw.at[d, both], intra)
@@ -276,30 +286,30 @@
         arrived(came, dst)
         send(name, dst, dst, sibling)
 
+    def piece(k, half):
+        return gall.at[k, :, span[half]]
+
+    def tiles(ch):
+        grad_tile(ch, across(z), across(y))
+        reduce_1(ch)
+        grad_tile(ch, up(z), up(y))
+        grad_tile(ch, down(z), down(y))
+        grad_tile(ch, z, y)
+
+    arrived("Xb", xrel.at[1])
+    send("Xb2", xrel.at[1], x2t.at[slot(od, oh, c)], intra_o)
+    send_g("Gi1", 1, intra)
     in_g.wait()
     in_w.wait()
     arrived("Gs", gall.at[slot(d, h, oc)])
     arrived("W", wsib)
-    act_half(d)
-    pass_on("Fi", "Gi", gall.at[slot(od, h, c)])
-    pass_on("Fx", "Gx", gall.at[slot(od, oh, c)])
+    act_part(d, 0, 8)
     arrived("Xa", xrel.at[0])
     send("Xa2", xrel.at[0], x2t.at[slot(od, h, c)], inter)
-    arrived("Xb", xrel.at[1])
-    send("Xb2", xrel.at[1], x2t.at[slot(od, oh, c)], intra_o)
-    most, rest = pl.ds(0, 384), pl.ds(384, 128)
-    send("Ga", gall.at[slot(od, h, c), most], gall.at[slot(od, h, c), most], inter)
-    send("Gb", gall.at[slot(od, oh, c), rest], gall.at[slot(od, oh, c), rest], intra)
-    arrived("Fi", gall.at[slot(od, h, oc)])
-    act_half(od)
-
-    send("Pd1", pbuf.at[d, 2 * oh + oc], arel.at[1], inter)
-    send("Pd0", pbuf.at[d, 2 * oh + c], arel.at[0], intra)
-    send("Pb0", pbuf.at[od, 2 * h + c], actr.at[me], intra)
-    send("Pb1", pbuf.at[od, 2 * h + oc], actr.at[me], intra_o)
-    send("Pc0", pbuf.at[od, 2 * oh + c], actr.at[me], inter)
-    send("Pc1", pbuf.at[od, 2 * oh + oc], actr.at[me], inter_o)
-    send("Pa", pbuf.at[d, 2 * h + oc], actr.at[me], sibling)
+    send_g("Gx1", 1, inter)
+    send_g("Gx0", 0, inter)
+    pass_on("Fi0", "Gi0", piece(slot(od, h, c), 0))
+    send("Ga", piece(slot(od, h, c), 0), piece(slot(od, h, c), 0), inter)
 
     own_x.wait()
     arrived("Xs", x2t.at[slot(d, h, oc)])
@@ -309,37 +319,61 @@
     arrived("Xx1", x2t.at[slot(od, oh, oc)])
     arrived("Xa2", x2t.at[slot(d, oh, c)])
     arrived("Xb2", x2t.at[slot(d, oh, oc)])
-
-    grad_tile(0, across(z), across(y))
-    reduce_1(0)
-    grad_tile(0, up(z), up(y))
-    grad_tile(0, down(z), down(y))
-    pass_on("Fb", "Gb", gall.at[slot(d, oh, c), rest])
-    grad_tile(0, z, y)
+    arrived("Fi0", piece(slot(od, h, oc), 0))
+    tiles(0)
+    pass_on("Fx1", "Gx1", piece(slot(od, oh, c), 1))
+    send("Gb", piece(slot(od, oh, c), 1), piece(slot(od, oh, c), 1), intra)
     reduce_2(0)
-    pass_on("Fa", "Ga", gall.at[slot(d, oh, c), most])
-    arrived("Fx", gall.at[slot(od, oh, oc)])
-    arrived("Fb", gall.at[slot(d, oh, oc), rest])
-    arrived("Fa", gall.at[slot(d, oh, oc), most])
-    grad_tile(1, across(z), across(y))
-    reduce_1(1)
+    send("Pd1", pbuf.at[d, 2 * oh + oc], arel.at[1], inter)
+    send("Pd0", pbuf.at[d, 2 * oh + c], arel.at[0], intra)
+    send("Pa", pbuf.at[d, 2 * h + oc], actr.at[me], sibling)
+
+    pass_on("Fi1", "Gi1", piece(slot(od, h, c), 1))
+    arrived("Fi1", piece(slot(od, h, oc), 1))
+    tiles(1)
     reduce_3(0)
-    grad_tile(1, up(z), up(y))
-    grad_tile(1, down(z), down(y))
+    act_part(od, 0, 2)
+    reduce_2(1)
+    pass_on("Fx0", "Gx0", piece(slot(od, oh, c), 0))
+    act_part(od, 2, 4)
     reduce_4(0)
-    grad_tile(1, z, y)
+    act_part(od, 4, 6)
+    pass_on("Fb", "Gb", piece(slot(d, oh, c), 1))
+    act_part(od, 6, 8)
+    send("Pb0", pbuf.at[od, 2 * h + c], actr.at[me], intra)
+    send("Pb1", pbuf.at[od, 2 * h + oc], actr.at[me], intra_o)
+    send("Pc0", pbuf.at[od, 2 * oh + c], actr.at[me], inter)
+    send("Pc1", pbuf.at[od, 2 * oh + oc], actr.at[me], inter_o)
+    pass_on("Fa", "Ga", piece(slot(d, oh, c), 0))
+    arrived("Fx1", piece(slot(od, oh, oc), 1))
+    arrived("Fb", piece(slot(d, oh, oc), 1))
+    tiles(3)
+    arrived("Fx0", piece(slot(od, oh, oc), 0))
+    arrived("Fa", piece(slot(d, oh, oc), 0))
+    grad_tile(2, across(z), across(y))
+    reduce_1(2)
+    reduce_3(1)
+    reduce_2(3)
+    grad_tile(2, up(z), up(y))
+    grad_tile(2, down(z), down(y))
+    grad_tile(2, z, y)
+    reduce_2(2)
+    reduce_4(1)
     arrived("Pd0", arel.at[0])
     send("Pf0", arel.at[0], actr.at[slot(od, h, c)], inter)
-    reduce_2(1)
+    hand_over(0)
     arrived("Pd1", arel.at[1])
     send("Pf1", arel.at[1], actr.at[slot(od, oh, c)], intra_o)
-    hand_over(0)
+    reduce_3(3)
+    hand_over(1)
+    reduce_3(2)
+    reduce_4(3)
+    reduce_4(2)
+    hand_over(3)
+    hand_over(2)
     in_ma.wait()
     in_mo.wait()
     in_se.wait()
-    reduce_3(1)
-    reduce_4(1)
-    hand_over(1)
     update()
 
     arrived("Pa", actr.at[slot(d, h, oc)])
@@ -430,14 +464,14 @@
             vm((2, 4, 128, 2048), BF16),
             vm((8, 128, 2048), BF16),
             vm((2, 128, 2048), BF16),
-            vm((2, 2, 4, 4, 64, 1024), BF16),
-            vm((2, 2, 2, 2, 64, 1024), BF16),
-            vm((2, 2, 2, 4, 64, 1024), BF16),
-            vm((2, 2, 4, 64, 1024), BF16),
-            vm((2, 2, 2, 32, 1024), BF16),
-            vm((2, 2, 2, 64, 1024), BF16),
-            vm((2, 2, 64, 1024), BF16),
-            vm((4, 64, 1024), BF16),
+            vm((4, 2, 4, 4, 64, 512), BF16),
+            vm((4, 2, 2, 2, 64, 512), BF16),
+            vm((4, 2, 2, 4, 64, 512), BF16),
+            vm((4, 2, 4, 64, 512), BF16),
+            vm((4, 2, 2, 32, 512), BF16),
+            vm((4, 2, 2, 64, 512), BF16),
+            vm((4, 2, 64, 512), BF16),
+            vm((4, 2, 64, 512), BF16),
             vm((4, 2048), F32),
             pltpu.SemaphoreType.DMA((COPIES,)),
             pltpu.SemaphoreType.DMA((COPIES,)),

time: 140 us -> 137 us (0.979); the launches traced: 138 us -> 137 us
  no operation moved by 1% of the time
where the time goes in v4:
time: 137 us
  Pallas kernels  137 us (100%)
    pallas_call x1, Pallas kernels, per_device(): pl.pallas_call(functools.partial(kernel, scale), out_shape=(vm((fine, fea...  134 us
    pallas_call x1, Pallas kernels, per_device(): pl.pallas_call(finish, out_shape=(jax.ShapeDtypeStruct((fine, features),...  2.91 us

profile of v4, /device:TPU:1, one launch (start us, length us, event | category | flops | bytes accessed | tf_op | source)
XLA Modules:
  0.0 137.3 jit_solution(9193673744590772033)
XLA Ops:
  0.6 133.6 %shard_map.101 = (bf16[512,2048]{1,0:T(8,128)(2,1)S(1)}, f32[4,2048]{1,0:T(4,128)S(1)}, f32[256,1024]{1,0:T(8,128)S(1)}, f32[256,1024]{1,0:T(8,128)S(1)}, f32[25...) custom-call(bf16[512,2048]{1,0:T(8,128)(2,1)} %bitcast.11, bf16[512,1024]{1,0:T(8,128)(2,1)} %bitcast.12, ...), custom_call_target="tpu_custom_call" | custom-call | tf_op jit(solution)/shard_map/pallas_call | solution.py:444
  134.2 2.9 %shard_map.102 = (bf16[512,2048]{1,0:T(8,128)(2,1)}, f32[256,1024]{1,0:T(8,128)}, f32[256,1024]{1,0:T(8,128)}, f32[256,1024]{1,0:T(8,128)}, bf16[2,256,1024]{2,1,0:T(8,128)(2,1)}) custom-call(bf16[512,2048]{1,0:T(8,128)(2,1)S(1)} %get-tuple-element.16.r_ref, f32[4,2048]{1,0:T(4,128)S(1)} %get-tuple-element.17.b_ref, f32[256,1024]{1,0:T(8,128)S(1)} %get-tuple-element.18.ma, ...), custom_call_target="tpu_custom_call" | custom-call | tf_op jit(solution)/shard_map/pallas_call | solution.py:484

commit v5 on v4

--- a/solution.py
+++ b/solution.py
@@ -121,6 +121,7 @@
         send(name, g_hbm.at[:, span[half]], gall.at[me, :, span[half]], device)
 
     send_g("Gi0", 0, intra)
+    send_g("Gx1", 1, inter)
     send("Gs", g_hbm, gall.at[me], sibling)
     send("W", w_hbm.at[oc], wsib, sibling)
 
@@ -258,29 +259,26 @@
             def _():
                 pltpu.make_async_copy(rsend.at[ch, i], home, recv_sem.at[mark]).start()
 
-    def update():
+    def update(half):
+        cols = slice(512 * half, 512 * half + 512)
         for j in range(SIDE):
             rows = slice(64 * j, 64 * j + 64)
-            for half in range(2):
-                mark = OWNED + 2 * j + half
-                pltpu.make_async_remote_copy(
-                    src_ref=gr.at[j, half], dst_ref=gr.at[j, half], send_sem=send_sem.at[mark],
-                    recv_sem=recv_sem.at[mark], device_id=sibling, device_id_type=MESH,
-                ).wait_recv()
-                cols = slice(512 * half, 512 * half + 512)
-                grad = wide(gr[j, half]) * scale
-                new_moment = first_beta * mo[rows, cols] + (1.0 - first_beta) * grad
-                new_second = second_beta * se[rows, cols] + (1.0 - second_beta) * grad * grad
-                ratio = new_moment / first_fix / (jnp.sqrt(new_second / second_fix) + adam_eps)
-                old = ma[rows, cols]
-                new_master = old - learn_rate * (ratio + weight_decay * old)
-                mo[rows, cols] = new_moment
-                se[rows, cols] = new_second
-                ma[rows, cols] = new_master
-                nw[d, rows, cols] = new_master.astype(BF16)
-            if j % 2 == 1:
-                both = pl.ds(64 * j - 64, 128)
-                send("nw" + str(j // 2), nw.at[d, both], nw.at[d, both], intra)
+            mark = OWNED + 2 * j + half
+            pltpu.make_async_remote_copy(
+                src_ref=gr.at[j, half], dst_ref=gr.at[j, half], send_sem=send_sem.at[mark],
+                recv_sem=recv_sem.at[mark], device_id=sibling, device_id_type=MESH,
+            ).wait_recv()
+            grad = wide(gr[j, half]) * scale
+            new_moment = first_beta * mo[rows, cols] + (1.0 - first_beta) * grad
+            new_second = second_beta * se[rows, cols] + (1.0 - second_beta) * grad * grad
+            ratio = new_moment / first_fix / (jnp.sqrt(new_second / second_fix) + adam_eps)
+            old = ma[rows, cols]
+            new_master = old - learn_rate * (ratio + weight_decay * old)
+            mo[rows, cols] = new_moment
+            se[rows, cols] = new_second
+            ma[rows, cols] = new_master
+            nw[d, rows, cols] = new_master.astype(BF16)
+        send("nw" + str(half), nw.at[d, :, span[half]], nw.at[d, :, span[half]], intra)
 
     def pass_on(name, came, dst):
         arrived(came, dst)
@@ -296,19 +294,20 @@
         grad_tile(ch, down(z), down(y))
         grad_tile(ch, z, y)
 
-    arrived("Xb", xrel.at[1])
-    send("Xb2", xrel.at[1], x2t.at[slot(od, oh, c)], intra_o)
-    send_g("Gi1", 1, intra)
     in_g.wait()
     in_w.wait()
     arrived("Gs", gall.at[slot(d, h, oc)])
     arrived("W", wsib)
     act_part(d, 0, 8)
+    arrived("Xb", xrel.at[1])
+    send("Xb2", xrel.at[1], x2t.at[slot(od, oh, c)], intra_o)
+    send_g("Gi1", 1, intra)
+    pass_on("Fi0", "Gi0", piece(slot(od, h, c), 0))
+    pass_on("Fx1", "Gx1", piece(slot(od, oh, c), 1))
+    send("Gb", piece(slot(od, oh, c), 1), piece(slot(od, oh, c), 1), intra)
     arrived("Xa", xrel.at[0])
     send("Xa2", xrel.at[0], x2t.at[slot(od, h, c)], inter)
-    send_g("Gx1", 1, inter)
     send_g("Gx0", 0, inter)
-    pass_on("Fi0", "Gi0", piece(slot(od, h, c), 0))
     send("Ga", piece(slot(od, h, c), 0), piece(slot(od, h, c), 0), inter)
 
     own_x.wait()
@@ -321,8 +320,6 @@
     arrived("Xb2", x2t.at[slot(d, oh, oc)])
     arrived("Fi0", piece(slot(od, h, oc), 0))
     tiles(0)
-    pass_on("Fx1", "Gx1", piece(slot(od, oh, c), 1))
-    send("Gb", piece(slot(od, oh, c), 1), piece(slot(od, oh, c), 1), intra)
     reduce_2(0)
     send("Pd1", pbuf.at[d, 2 * oh + oc], arel.at[1], inter)
     send("Pd0", pbuf.at[d, 2 * oh + c], arel.at[0], intra)
@@ -354,27 +351,28 @@
     reduce_1(2)
     reduce_3(1)
     reduce_2(3)
+    hand_over(0)
     grad_tile(2, up(z), up(y))
     grad_tile(2, down(z), down(y))
     grad_tile(2, z, y)
     reduce_2(2)
     reduce_4(1)
-    arrived("Pd0", arel.at[0])
-    send("Pf0", arel.at[0], actr.at[slot(od, h, c)], inter)
-    hand_over(0)
-    arrived("Pd1", arel.at[1])
-    send("Pf1", arel.at[1], actr.at[slot(od, oh, c)], intra_o)
     reduce_3(3)
     hand_over(1)
-    reduce_3(2)
     reduce_4(3)
-    reduce_4(2)
-    hand_over(3)
-    hand_over(2)
     in_ma.wait()
     in_mo.wait()
     in_se.wait()
-    update()
+    hand_over(3)
+    reduce_3(2)
+    reduce_4(2)
+    hand_over(2)
+    arrived("Pd1", arel.at[1])
+    send("Pf1", arel.at[1], actr.at[slot(od, oh, c)], intra_o)
+    arrived("Pd0", arel.at[0])
+    send("Pf0", arel.at[0], actr.at[slot(od, h, c)], inter)
+    update(1)
+    update(0)
 
     arrived("Pa", actr.at[slot(d, h, oc)])
     arrived("Pb0", actr.at[slot(od, h, c)])
@@ -392,7 +390,7 @@
     send("bnd", bsend, brecv, prev_dev)
     arrived("bnd", brecv)
     for j in range(2):
-        arrived("nw" + str(j), nw.at[od, pl.ds(128 * j, 128)])
+        arrived("nw" + str(j), nw.at[od, :, span[j]])
     for mine, copy in maybe:
 
         @pl.when(jnp.logical_not(mine))

time: 137 us -> 142 us (1.036)
  Pallas kernels: 137 us -> 141 us
    pallas_call x1, Pallas kernels: 134 us -> 138 us  [per_device(): pl.pallas_call(functools.partial(kernel, scale), out_shape=(vm((fine, fea...]
where the time goes in v5:
time: 142 us
  Pallas kernels  141 us (99%)
    pallas_call x1, Pallas kernels, per_device(): pl.pallas_call(functools.partial(kernel, scale), out_shape=(vm((fine, fea...  138 us
    pallas_call x1, Pallas kernels, per_device(): pl.pallas_call(finish, out_shape=(jax.ShapeDtypeStruct((fine, features),...  2.92 us

profile of v5, /device:TPU:1, one launch (start us, length us, event | category | flops | bytes accessed | tf_op | source)
XLA Modules:
  0.0 142.1 jit_solution(13122739412501576133)
XLA Ops:
  0.6 138.4 %shard_map.101 = (bf16[512,2048]{1,0:T(8,128)(2,1)S(1)}, f32[4,2048]{1,0:T(4,128)S(1)}, f32[256,1024]{1,0:T(8,128)S(1)}, f32[256,1024]{1,0:T(8,128)S(1)}, f32[25...) custom-call(bf16[512,2048]{1,0:T(8,128)(2,1)} %bitcast.11, bf16[512,1024]{1,0:T(8,128)(2,1)} %bitcast.12, ...), custom_call_target="tpu_custom_call" | custom-call | tf_op jit(solution)/shard_map/pallas_call | solution.py:442
  139.0 2.9 %shard_map.102 = (bf16[512,2048]{1,0:T(8,128)(2,1)}, f32[256,1024]{1,0:T(8,128)}, f32[256,1024]{1,0:T(8,128)}, f32[256,1024]{1,0:T(8,128)}, bf16[2,256,1024]{2,1,0:T(8,128)(2,1)}) custom-call(bf16[512,2048]{1,0:T(8,128)(2,1)S(1)} %get-tuple-element.16.r_ref, f32[4,2048]{1,0:T(4,128)S(1)} %get-tuple-element.17.b_ref, f32[256,1024]{1,0:T(8,128)S(1)} %get-tuple-element.18.ma, ...), custom_call_target="tpu_custom_call" | custom-call | tf_op jit(solution)/shard_map/pallas_call | solution.py:482

commit v6 on v5

--- a/solution.py
+++ b/solution.py
@@ -121,7 +121,6 @@
         send(name, g_hbm.at[:, span[half]], gall.at[me, :, span[half]], device)
 
     send_g("Gi0", 0, intra)
-    send_g("Gx1", 1, inter)
     send("Gs", g_hbm, gall.at[me], sibling)
     send("W", w_hbm.at[oc], wsib, sibling)
 
@@ -294,20 +293,19 @@
         grad_tile(ch, down(z), down(y))
         grad_tile(ch, z, y)
 
+    arrived("Xb", xrel.at[1])
+    send("Xb2", xrel.at[1], x2t.at[slot(od, oh, c)], intra_o)
+    send_g("Gi1", 1, intra)
     in_g.wait()
     in_w.wait()
     arrived("Gs", gall.at[slot(d, h, oc)])
     arrived("W", wsib)
     act_part(d, 0, 8)
-    arrived("Xb", xrel.at[1])
-    send("Xb2", xrel.at[1], x2t.at[slot(od, oh, c)], intra_o)
-    send_g("Gi1", 1, intra)
-    pass_on("Fi0", "Gi0", piece(slot(od, h, c), 0))
-    pass_on("Fx1", "Gx1", piece(slot(od, oh, c), 1))
-    send("Gb", piece(slot(od, oh, c), 1), piece(slot(od, oh, c), 1), intra)
     arrived("Xa", xrel.at[0])
     send("Xa2", xrel.at[0], x2t.at[slot(od, h, c)], inter)
+    send_g("Gx1", 1, inter)
     send_g("Gx0", 0, inter)
+    pass_on("Fi0", "Gi0", piece(slot(od, h, c), 0))
     send("Ga", piece(slot(od, h, c), 0), piece(slot(od, h, c), 0), inter)
 
     own_x.wait()
@@ -320,6 +318,8 @@
     arrived("Xb2", x2t.at[slot(d, oh, oc)])
     arrived("Fi0", piece(slot(od, h, oc), 0))
     tiles(0)
+    pass_on("Fx1", "Gx1", piece(slot(od, oh, c), 1))
+    send("Gb", piece(slot(od, oh, c), 1), piece(slot(od, oh, c), 1), intra)
     reduce_2(0)
     send("Pd1", pbuf.at[d, 2 * oh + oc], arel.at[1], inter)
     send("Pd0", pbuf.at[d, 2 * oh + c], arel.at[0], intra)
@@ -357,6 +357,10 @@
     grad_tile(2, z, y)
     reduce_2(2)
     reduce_4(1)
+    arrived("Pd1", arel.at[1])
+    send("Pf1", arel.at[1], actr.at[slot(od, oh, c)], intra_o)
+    arrived("Pd0", arel.at[0])
+    send("Pf0", arel.at[0], actr.at[slot(od, h, c)], inter)
     reduce_3(3)
     hand_over(1)
     reduce_4(3)
@@ -367,10 +371,6 @@
     reduce_3(2)
     reduce_4(2)
     hand_over(2)
-    arrived("Pd1", arel.at[1])
-    send("Pf1", arel.at[1], actr.at[slot(od, oh, c)], intra_o)
-    arrived("Pd0", arel.at[0])
-    send("Pf0", arel.at[0], actr.at[slot(od, h, c)], inter)
     update(1)
     update(0)
 

time: 142 us -> 137 us (0.965)
  Pallas kernels: 141 us -> 136 us
    pallas_call x1, Pallas kernels: 138 us -> 133 us  [per_device(): pl.pallas_call(functools.partial(kernel, scale), out_shape=(vm((fine, fea...]
where the time goes in v6:
time: 137 us
  Pallas kernels  136 us (99%)
    pallas_call x1, Pallas kernels, per_device(): pl.pallas_call(functools.partial(kernel, scale), out_shape=(vm((fine, fea...  133 us
    pallas_call x1, Pallas kernels, per_device(): pl.pallas_call(finish, out_shape=(jax.ShapeDtypeStruct((fine, features),...  2.92 us

profile of v6, /device:TPU:1, one launch (start us, length us, event | category | flops | bytes accessed | tf_op | source)
XLA Modules:
  0.0 136.6 jit_solution(9176885630340243686)
XLA Ops:
  0.6 132.9 %shard_map.101 = (bf16[512,2048]{1,0:T(8,128)(2,1)S(1)}, f32[4,2048]{1,0:T(4,128)S(1)}, f32[256,1024]{1,0:T(8,128)S(1)}, f32[256,1024]{1,0:T(8,128)S(1)}, f32[25...) custom-call(bf16[512,2048]{1,0:T(8,128)(2,1)} %bitcast.11, bf16[512,1024]{1,0:T(8,128)(2,1)} %bitcast.12, ...), custom_call_target="tpu_custom_call" | custom-call | tf_op jit(solution)/shard_map/pallas_call | solution.py:442
  133.5 2.9 %shard_map.102 = (bf16[512,2048]{1,0:T(8,128)(2,1)}, f32[256,1024]{1,0:T(8,128)}, f32[256,1024]{1,0:T(8,128)}, f32[256,1024]{1,0:T(8,128)}, bf16[2,256,1024]{2,1,0:T(8,128)(2,1)}) custom-call(bf16[512,2048]{1,0:T(8,128)(2,1)S(1)} %get-tuple-element.16.r_ref, f32[4,2048]{1,0:T(4,128)S(1)} %get-tuple-element.17.b_ref, f32[256,1024]{1,0:T(8,128)S(1)} %get-tuple-element.18.ma, ...), custom_call_target="tpu_custom_call" | custom-call | tf_op jit(solution)/shard_map/pallas_call | solution.py:482

commit v7 on v6

--- a/solution.py
+++ b/solution.py
@@ -286,6 +286,9 @@
     def piece(k, half):
         return gall.at[k, :, span[half]]
 
+    def quarter(k, part):
+        return gall.at[k, pl.ds(256 * part, 256), span[1]]
+
     def tiles(ch):
         grad_tile(ch, across(z), across(y))
         reduce_1(ch)
@@ -319,13 +322,14 @@
     arrived("Fi0", piece(slot(od, h, oc), 0))
     tiles(0)
     pass_on("Fx1", "Gx1", piece(slot(od, oh, c), 1))
-    send("Gb", piece(slot(od, oh, c), 1), piece(slot(od, oh, c), 1), intra)
+    send("Gb", quarter(slot(od, oh, c), 0), quarter(slot(od, oh, c), 0), intra)
     reduce_2(0)
-    send("Pd1", pbuf.at[d, 2 * oh + oc], arel.at[1], inter)
     send("Pd0", pbuf.at[d, 2 * oh + c], arel.at[0], intra)
     send("Pa", pbuf.at[d, 2 * h + oc], actr.at[me], sibling)
 
     pass_on("Fi1", "Gi1", piece(slot(od, h, c), 1))
+    send("Ga2", quarter(slot(od, h, c), 1), quarter(slot(od, h, c), 1), inter)
+    send("Pd1", pbuf.at[d, 2 * oh + oc], arel.at[1], inter)
     arrived("Fi1", piece(slot(od, h, oc), 1))
     tiles(1)
     reduce_3(0)
@@ -335,44 +339,46 @@
     act_part(od, 2, 4)
     reduce_4(0)
     act_part(od, 4, 6)
-    pass_on("Fb", "Gb", piece(slot(d, oh, c), 1))
+    pass_on("Fb", "Gb", quarter(slot(d, oh, c), 0))
     act_part(od, 6, 8)
     send("Pb0", pbuf.at[od, 2 * h + c], actr.at[me], intra)
     send("Pb1", pbuf.at[od, 2 * h + oc], actr.at[me], intra_o)
     send("Pc0", pbuf.at[od, 2 * oh + c], actr.at[me], inter)
     send("Pc1", pbuf.at[od, 2 * oh + oc], actr.at[me], inter_o)
     pass_on("Fa", "Ga", piece(slot(d, oh, c), 0))
-    arrived("Fx1", piece(slot(od, oh, oc), 1))
-    arrived("Fb", piece(slot(d, oh, oc), 1))
-    tiles(3)
     arrived("Fx0", piece(slot(od, oh, oc), 0))
     arrived("Fa", piece(slot(d, oh, oc), 0))
-    grad_tile(2, across(z), across(y))
-    reduce_1(2)
+    tiles(2)
+    pass_on("Fa2", "Ga2", quarter(slot(d, oh, c), 1))
+    arrived("Fx1", piece(slot(od, oh, oc), 1))
+    arrived("Fb", quarter(slot(d, oh, oc), 0))
+    arrived("Fa2", quarter(slot(d, oh, oc), 1))
+    grad_tile(3, across(z), across(y))
+    reduce_1(3)
     reduce_3(1)
+    reduce_2(2)
+    hand_over(0)
+    grad_tile(3, up(z), up(y))
+    grad_tile(3, down(z), down(y))
+    grad_tile(3, z, y)
     reduce_2(3)
-    hand_over(0)
-    grad_tile(2, up(z), up(y))
-    grad_tile(2, down(z), down(y))
-    grad_tile(2, z, y)
-    reduce_2(2)
     reduce_4(1)
     arrived("Pd1", arel.at[1])
     send("Pf1", arel.at[1], actr.at[slot(od, oh, c)], intra_o)
     arrived("Pd0", arel.at[0])
     send("Pf0", arel.at[0], actr.at[slot(od, h, c)], inter)
-    reduce_3(3)
+    reduce_3(2)
     hand_over(1)
-    reduce_4(3)
+    reduce_4(2)
     in_ma.wait()
     in_mo.wait()
     in_se.wait()
+    hand_over(2)
+    reduce_3(3)
+    reduce_4(3)
     hand_over(3)
-    reduce_3(2)
-    reduce_4(2)
-    hand_over(2)
+    update(0)
     update(1)
-    update(0)
 
     arrived("Pa", actr.at[slot(d, h, oc)])
     arrived("Pb0", actr.at[slot(od, h, c)])

time: 137 us -> 138 us (level)
  Pallas kernels: 136 us -> 138 us
    pallas_call x1, Pallas kernels: 133 us -> 135 us  [per_device(): pl.pallas_call(functools.partial(kernel, scale), out_shape=(vm((fine, fea...]
where the time goes in v7:
time: 138 us
  Pallas kernels  138 us (100%)
    pallas_call x1, Pallas kernels, per_device(): pl.pallas_call(functools.partial(kernel, scale), out_shape=(vm((fine, fea...  135 us
    pallas_call x1, Pallas kernels, per_device(): pl.pallas_call(finish, out_shape=(jax.ShapeDtypeStruct((fine, features),...  2.92 us

profile of v7, /device:TPU:1, one launch (start us, length us, event | category | flops | bytes accessed | tf_op | source)
XLA Modules:
  0.0 138.4 jit_solution(61714719008028300)
XLA Ops:
  0.6 134.6 %shard_map.101 = (bf16[512,2048]{1,0:T(8,128)(2,1)S(1)}, f32[4,2048]{1,0:T(4,128)S(1)}, f32[256,1024]{1,0:T(8,128)S(1)}, f32[256,1024]{1,0:T(8,128)S(1)}, f32[25...) custom-call(bf16[512,2048]{1,0:T(8,128)(2,1)} %bitcast.11, bf16[512,1024]{1,0:T(8,128)(2,1)} %bitcast.12, ...), custom_call_target="tpu_custom_call" | custom-call | tf_op jit(solution)/shard_map/pallas_call | solution.py:448
  135.3 2.9 %shard_map.102 = (bf16[512,2048]{1,0:T(8,128)(2,1)}, f32[256,1024]{1,0:T(8,128)}, f32[256,1024]{1,0:T(8,128)}, f32[256,1024]{1,0:T(8,128)}, bf16[2,256,1024]{2,1,0:T(8,128)(2,1)}) custom-call(bf16[512,2048]{1,0:T(8,128)(2,1)S(1)} %get-tuple-element.16.r_ref, f32[4,2048]{1,0:T(4,128)S(1)} %get-tuple-element.17.b_ref, f32[256,1024]{1,0:T(8,128)S(1)} %get-tuple-element.18.ma, ...), custom_call_target="tpu_custom_call" | custom-call | tf_op jit(solution)/shard_map/pallas_call | solution.py:488
